TPU v7x, 256 devices: a whole 4x4x8 slice. The times are simulated.
256 devices in a mesh: tile: 64 (over x, z, core), aux: 4 (over y).
Axes of the slice: x: 4, y: 4, z: 8, core: 2. Of those that a mesh axis runs over, the one named last changes fastest.
Arguments:
- density: float32 [8192, 8192], P('tile', 'aux'), may hold values from -6 to 6
- factors: float32 [1536, 16, 128, 128], P(('tile', 'aux')), may hold values from -0.125 to 0.125
- orthogonalizers: float32 [8192, 128], replicated, may hold values from -0.5 to 0.5
- slot_pairs: int32 [8192, 2], P(('tile', 'aux')), may hold values from 0 to 5
- density_source: int32 [8192, 1], replicated, may hold values from 0 to 63; in each aligned block of 32 rows (0 to 31, 32 to 63, ...) at most 2 rows name the same one
- density_column: int32 [8192, 1], replicated, may hold values from 0 to 63
- target_row: int32 [8192, 1], replicated, may hold values from 0 to 63; in each aligned block of 32 rows (0 to 31, 32 to 63, ...) at most 2 rows name the same one
- target_column: int32 [8192, 1], replicated, may hold values from 0 to 63
Outputs:
- fock_exchange: float32 [8192, 8192], P('tile', 'aux')
Inputs may be any that keep to these rules, and one draw needn't show every extreme that they name: `density_source`: in each aligned block of 32 rows (the tasks of one device) no row tile is named more than 2 times, a bound that some block reaches. `target_row`: in each aligned block of 32 rows (the tasks of one device) no row tile is named more than 2 times, a bound that some block reaches.
All inputs are finite; a program needn't handle non-finite values.
Results may differ from a plain program's by a relative error of at most 0.0001.
Values sent between devices are 32-bit elements; how exact they have to be, the bound alone decides.
A program may use at most 128 MiB of HBM per device.

v0:
```python
import jax
import jax.numpy as jnp
from jax import lax
from jax.sharding import PartitionSpec as P

highest = lax.Precision.HIGHEST


def ranks_of(key_rows):
    task_count = key_rows.shape[-1]
    position = jnp.arange(task_count)
    earlier = position[None, :] < position[:, None]
    matching = key_rows[..., :, None] == key_rows[..., None, :]
    return jnp.sum(matching & earlier, axis=-1)


def slot_table(key_rows, other_rows, wanted, capacity):
    ranking = ranks_of(key_rows)
    levels = jnp.arange(capacity)
    chosen = (key_rows == wanted)[..., None, :] & (ranking[..., None, :] == levels[:, None])
    picked = jnp.sum(jnp.where(chosen, other_rows[..., None, :], 0), axis=-1)
    filled = jnp.any(chosen, axis=-1)
    return (picked, filled)


def local(
    density,
    factors,
    orthogonalizers,
    slot_pairs,
    density_source,
    density_column,
    target_row,
    target_column,
):
    tiles_all = lax.axis_size("tile")
    aux_count = lax.axis_size("aux")
    tile_me = lax.axis_index("tile")
    aux_me = lax.axis_index("aux")
    tile_width = factors.shape[-1]
    task_count = slot_pairs.shape[0]
    capacity = max(2, 2 * task_count // tiles_all)
    quarter = tile_width // aux_count
    per_block = tiles_all // aux_count
    source_grid = density_source.reshape(tiles_all, aux_count, task_count)
    column_grid = density_column.reshape(tiles_all, aux_count, task_count)
    target_grid = target_row.reshape(tiles_all, aux_count, task_count)
    target_cols = target_column.reshape(tiles_all, aux_count, task_count)
    own_source = source_grid[tile_me, aux_me]
    own_target = target_grid[tile_me, aux_me]
    row_slab = lax.all_gather(density, "aux", axis=1, tiled=True)
    slab_tiles = row_slab.reshape(tile_width, tiles_all, tile_width)
    group_source = lax.dynamic_index_in_dim(source_grid, aux_me, 1, False)
    group_column = lax.dynamic_index_in_dim(column_grid, aux_me, 1, False)
    send_cols, send_filled = slot_table(group_source, group_column, tile_me, capacity)
    outgoing = jnp.take(slab_tiles, send_cols, axis=1)
    outgoing = jnp.where(send_filled[None, :, :, None], outgoing, 0.0)
    incoming = lax.all_to_all(outgoing, "tile", split_axis=1, concat_axis=1, tiled=True)
    own_rank = ranks_of(own_source)
    group = 8
    batches = task_count // group

    def one_batch(items):
        sources, rank_block, lefts, rights = items
        dens_block = incoming[:, sources, rank_block, :]
        halfway = jnp.einsum("gpik,kgl->gpil", factors[lefts], dens_block, precision=highest)
        return jnp.einsum("gpil,gplj->gij", halfway, factors[rights], precision=highest)

    partials = lax.map(
        one_batch,
        (
            own_source.reshape(batches, group),
            own_rank.reshape(batches, group),
            slot_pairs[:, 0].reshape(batches, group),
            slot_pairs[:, 1].reshape(batches, group),
        ),
    )
    partials = partials.reshape(task_count, tile_width, tile_width)
    task_ids = jnp.arange(task_count, dtype=jnp.int32)
    owners = jnp.arange(tiles_all, dtype=jnp.int32)[:, None]
    send_task, send_live = slot_table(own_target[None, :], task_ids[None, :], owners, capacity)
    outbound = jnp.where(send_live[:, :, None, None], partials[send_task], 0.0)
    arrived = lax.all_to_all(outbound, "tile", split_axis=0, concat_axis=0, tiled=True)
    group_target = lax.dynamic_index_in_dim(target_grid, aux_me, 1, False)
    group_cols = lax.dynamic_index_in_dim(target_cols, aux_me, 1, False)
    cols_b, cols_live = slot_table(group_target, group_cols, tile_me, capacity)
    spread = ((cols_b.reshape(-1)[None, :] == owners) & cols_live.reshape(-1)[None, :]).astype(
        jnp.float32
    )
    row_sums = jnp.einsum(
        "bs,sij->ibj", spread, arrived.reshape(-1, tile_width, tile_width), precision=highest
    )
    row_sums = row_sums.reshape(tile_width, tiles_all * tile_width)
    exchange_rows = lax.psum_scatter(row_sums, "aux", scatter_dimension=0, tiled=True)
    mirrored = lax.all_to_all(
        lax.all_to_all(
            exchange_rows.reshape(quarter, tiles_all, tile_width),
            "tile",
            split_axis=1,
            concat_axis=1,
            tiled=True,
        ),
        "aux",
        split_axis=1,
        concat_axis=0,
        tiled=True,
    )
    full_rows = lax.all_to_all(
        exchange_rows.reshape(quarter, aux_count, per_block * tile_width),
        "aux",
        split_axis=1,
        concat_axis=0,
        tiled=True,
    )
    direct_part = full_rows.reshape(tile_width, per_block, tile_width)
    symmetric = direct_part + jnp.transpose(mirrored, (2, 1, 0))
    blocks_x = orthogonalizers.reshape(tiles_all, tile_width, tile_width)
    left_x = blocks_x[tile_me]
    right_x = lax.dynamic_slice_in_dim(blocks_x, aux_me * per_block, per_block, 0)
    leftward = jnp.einsum("ki,kbl->ibl", left_x, symmetric, precision=highest)
    fock = jnp.einsum("ibl,blj->ibj", leftward, right_x, precision=highest)
    return fock.reshape(tile_width, per_block * tile_width)


def solution(mesh):
    return jax.shard_map(
        local,
        mesh=mesh,
        in_specs=(
            P("tile", "aux"),
            P(("tile", "aux"), None, None, None),
            P(),
            P(("tile", "aux"), None),
            P(),
            P(),
            P(),
            P(),
        ),
        out_specs=P("tile", "aux"),
        check_vma=False,
    )
```

profile of v0, /device:TPU:22, one launch (start us, length us, event | category | flops | bytes accessed | tf_op | source)
XLA Modules:
  0.0 803.1 jit_solution(7440394186172152898)
XLA Ops:
  6.5 2.5 copy.132
  11.3 1.5 reduce.27
  13.0 1.5 reduce.26
  16.0 45.8 %all-gather.2.cloned.1.call-done = f32[128,8192]{0,1:T(8,128)} async-done(((f32[128,2048]{0,1:T(8,128)}), f32[128,8192]{0,1:T(8,128)}) %all-gather.2.cloned.1.call-update) | async-done | bytes 4194320 | tf_op jit(solution)/shard_map/all_gather | solution.py:51
  61.9 5.6 copy.134
  67.5 6.5 gather_fusion.3
  73.9 5.9 select_bitcast_fusion
  79.9 11.1 %all-to-all-start = ((f32[128,64,2,128]{3,0,2,1:T(8,128)}), f32[128,64,2,128]{3,0,2,1:T(8,128)}, u32[]{:S(2)}, u32[]{:S(2)}) async-start(f32[128,64,2,128]{3,0,2,1:T(8,128)} %select_bitcast_fusion), calls=%async_computation | async-start | bytes 16777216 | tf_op jit(solution)/shard_map/all_to_all | solution.py:58
  92.0 182.3 %all-to-all-done = f32[128,64,2,128]{3,0,2,1:T(8,128)} async-done(((f32[128,64,2,128]{3,0,2,1:T(8,128)}), f32[128,64,2,128]{3,0,2,1:T(8,128)}, u32[]{:S(2)}, u32[]{:S(2)}) %all-to-all-start) | async-done | bytes 8388640 | tf_op jit(solution)/shard_map/all_to_all | solution.py:58
  274.3 164.1 %while.10 = (s32[]{:T(128)}, f32[4,8,128,128]{3,2,1,0:T(8,128)S(1)}, s32[4,8]{1,0:T(4,128)S(1)}, f32[6,16,128,128]{3,2,1,0:T(8,128)}, s32[4,8]{1,0:T(4,128)S(1)}...) while((s32[]{:T(128)}, f32[4,8,128,128]{3,2,1,0:T(8,128)S(1)}, ...), condition=%wide.region_7.8_spmd, body=%wide.region_6.7_spmd.sunk | while | flops 6442452992 | bytes 69214728 | solution.py:69
  274.3 7.1 gather_fusion
  281.4 4.0 gather_fusion.1
  285.4 11.0 %fusion.49 = f32[8,16,128,128]{3,2,1,0:T(8,128)} fusion(f32[8,16,128,128]{3,2,1,0:T(8,128)} %gather_fusion, f32[8,128,128]{2,1,0:T(8,128)S(1)} %gather_fusion.1), kind=kOutput, calls=%fused_computation.7.clone.1 | convolution fusion | flops 3221225472 | bytes 17301504 | tf_op jit(solution)/shard_map/while/body/eval_jaxpr/gpik,kgl->gpil/dot_general | solution.py:66
  296.4 7.1 gather_fusion.2
  303.5 11.8 %fusion.51 = f32[4,8,128,128]{3,2,1,0:T(8,128)S(1)} fusion(f32[4,8,128,128]{3,2,1,0:T(8,128)S(1)} %get-tuple-element.139, s32[]{:T(128)} %get-tuple-element.138, f32[8,16,128,128]{3,2,1,0:T(8,128)} %fusion.49, f32[8,16,128,128]{3,2,1,0:T(8,128)} %gather_fusion.2), kind=kOutput, calls=%fused_computation.6.clone.1 | convolution fusion | flops 3221225472 | bytes 17301508 | tf_op jit(solution)/shard_map/while/body/eval_jaxpr/gpil,gplj->gij/dot_general | solution.py:67
  315.3 7.1 gather_fusion
  322.4 4.0 gather_fusion.1
  326.4 11.0 %fusion.49 = f32[8,16,128,128]{3,2,1,0:T(8,128)} fusion(f32[8,16,128,128]{3,2,1,0:T(8,128)} %gather_fusion, f32[8,128,128]{2,1,0:T(8,128)S(1)} %gather_fusion.1), kind=kOutput, calls=%fused_computation.7.clone.1 | convolution fusion | flops 3221225472 | bytes 17301504 | tf_op jit(solution)/shard_map/while/body/eval_jaxpr/gpik,kgl->gpil/dot_general | solution.py:66
  337.4 7.1 gather_fusion.2
  344.5 11.8 %fusion.51 = f32[4,8,128,128]{3,2,1,0:T(8,128)S(1)} fusion(f32[4,8,128,128]{3,2,1,0:T(8,128)S(1)} %get-tuple-element.139, s32[]{:T(128)} %get-tuple-element.138, f32[8,16,128,128]{3,2,1,0:T(8,128)} %fusion.49, f32[8,16,128,128]{3,2,1,0:T(8,128)} %gather_fusion.2), kind=kOutput, calls=%fused_computation.6.clone.1 | convolution fusion | flops 3221225472 | bytes 17301508 | tf_op jit(solution)/shard_map/while/body/eval_jaxpr/gpil,gplj->gij/dot_general | solution.py:67
  356.4 7.1 gather_fusion
  363.4 4.0 gather_fusion.1
  367.4 11.0 %fusion.49 = f32[8,16,128,128]{3,2,1,0:T(8,128)} fusion(f32[8,16,128,128]{3,2,1,0:T(8,128)} %gather_fusion, f32[8,128,128]{2,1,0:T(8,128)S(1)} %gather_fusion.1), kind=kOutput, calls=%fused_computation.7.clone.1 | convolution fusion | flops 3221225472 | bytes 17301504 | tf_op jit(solution)/shard_map/while/body/eval_jaxpr/gpik,kgl->gpil/dot_general | solution.py:66
  378.4 7.1 gather_fusion.2
  385.5 11.8 %fusion.51 = f32[4,8,128,128]{3,2,1,0:T(8,128)S(1)} fusion(f32[4,8,128,128]{3,2,1,0:T(8,128)S(1)} %get-tuple-element.139, s32[]{:T(128)} %get-tuple-element.138, f32[8,16,128,128]{3,2,1,0:T(8,128)} %fusion.49, f32[8,16,128,128]{3,2,1,0:T(8,128)} %gather_fusion.2), kind=kOutput, calls=%fused_computation.6.clone.1 | convolution fusion | flops 3221225472 | bytes 17301508 | tf_op jit(solution)/shard_map/while/body/eval_jaxpr/gpil,gplj->gij/dot_general | solution.py:67
  397.4 7.1 gather_fusion
  404.5 4.0 gather_fusion.1
  408.4 11.0 %fusion.49 = f32[8,16,128,128]{3,2,1,0:T(8,128)} fusion(f32[8,16,128,128]{3,2,1,0:T(8,128)} %gather_fusion, f32[8,128,128]{2,1,0:T(8,128)S(1)} %gather_fusion.1), kind=kOutput, calls=%fused_computation.7.clone.1 | convolution fusion | flops 3221225472 | bytes 17301504 | tf_op jit(solution)/shard_map/while/body/eval_jaxpr/gpik,kgl->gpil/dot_general | solution.py:66
  419.5 7.1 gather_fusion.2
  426.5 11.8 %fusion.51 = f32[4,8,128,128]{3,2,1,0:T(8,128)S(1)} fusion(f32[4,8,128,128]{3,2,1,0:T(8,128)S(1)} %get-tuple-element.139, s32[]{:T(128)} %get-tuple-element.138, f32[8,16,128,128]{3,2,1,0:T(8,128)} %fusion.49, f32[8,16,128,128]{3,2,1,0:T(8,128)} %gather_fusion.2), kind=kOutput, calls=%fused_computation.6.clone.1 | convolution fusion | flops 3221225472 | bytes 17301508 | tf_op jit(solution)/shard_map/while/body/eval_jaxpr/gpil,gplj->gij/dot_general | solution.py:67
  438.4 4.3 gather_fusion.4
  442.7 7.2 broadcast_select_fusion
  449.9 8.7 %all-to-all-start.1 = ((f32[64,2,128,128]{3,2,1,0:T(8,128)}), f32[64,2,128,128]{3,2,1,0:T(8,128)}, u32[]{:S(2)}, u32[]{:S(2)}) async-start(f32[64,2,128,128]{3,2,1,0:T(8,128)} %broadcast_select_fusion), calls=%async_computation.1 | async-start | bytes 16777216 | tf_op jit(solution)/shard_map/all_to_all | solution.py:83
  460.3 181.6 %all-to-all-done.1 = f32[64,2,128,128]{3,2,1,0:T(8,128)} async-done(((f32[64,2,128,128]{3,2,1,0:T(8,128)}), f32[64,2,128,128]{3,2,1,0:T(8,128)}, u32[]{:S(2)}, u32[]{:S(2)}) %all-to-all-start.1) | async-done | bytes 8388640 | tf_op jit(solution)/shard_map/all_to_all | solution.py:83
  641.9 12.2 %copy.136 = f32[64,2,128,128]{3,1,0,2:T(2,128)S(1)} copy(f32[64,2,128,128]{3,2,1,0:T(8,128)} %all-to-all-done.1) | data formatting | bytes 16777216 | tf_op jit(solution)/shard_map/all_to_all | solution.py:83
  654.1 3.7 fusion.22
  657.9 5.2 copy.163
  663.1 46.9 %reduce-scatter.2.cloned.1.call-done = f32[32,8192]{1,0:T(8,128)} async-done(((f32[128,8192]{1,0:T(8,128)}), f32[32,8192]{1,0:T(8,128)}) %reduce-scatter.2.cloned.1.call-update) | async-done | bytes 1048592 | tf_op jit(solution)/shard_map/reduce_scatter | solution.py:94
  710.0 2.3 copy.164
  712.3 5.5 all-to-all-start.2
  719.2 11.1 %all-to-all-done.2 = f32[32,4,2048]{2,0,1:T(8,128)S(1)} async-done(((f32[32,4,2048]{2,0,1:T(8,128)}), f32[32,4,2048]{2,0,1:T(8,128)S(1)}, u32[]{:S(2)}, u32[]{:S(2)}) %all-to-all-start.2) | async-done | bytes 1048608 | tf_op jit(solution)/shard_map/all_to_all | solution.py:108
  730.3 37.3 %all_to_all.48 = f32[32,64,128]{2,0,1:T(8,128)} all-to-all(f32[32,64,128]{2,0,1:T(8,128)S(1)} %copy_bitcast_fusion.1), channel_id=1, replica_groups=mesh['tile'=64,'aux'=4] {'tile'}, dimensions={1} | all-to-all | bytes 2097152 | tf_op jit(solution)/shard_map/all_to_all | solution.py:96
  767.6 6.5 all-to-all-start.4
  774.2 11.9 %all-to-all-done.4 = f32[32,64,128]{2,0,1:T(8,128)S(1)} async-done(((f32[32,64,128]{2,0,1:T(8,128)}), f32[32,64,128]{2,0,1:T(8,128)S(1)}, u32[]{:S(2)}, u32[]{:S(2)}) %all-to-all-start.4) | async-done | bytes 1048608 | tf_op jit(solution)/shard_map/all_to_all | solution.py:95
  786.1 1.6 copy.144
  787.7 1.8 copy.145
  789.7 2.1 fusion.9
  791.9 3.1 fusion.11
  (79 shorter events, 9.8 us)
Async XLA Ops:
  6.5 55.3 %all-gather.2.cloned.1.call-start = ((), (), s32[]{:S(2)}) async-start(), calls=%async_computation.6 | async-start | bytes 5242880 | tf_op jit(solution)/shard_map/all_gather | solution.py:51
  79.9 11.5 %copy-start.1 = (s32[32,2]{0,1:T(2,128)S(1)}, s32[32,2]{0,1:T(2,128)}, u32[]{:S(2)}) copy-start(s32[32,2]{0,1:T(2,128)} %param.13) | copy-start | bytes 772
  79.9 194.4 %all-to-all-start = ((f32[128,64,2,128]{3,0,2,1:T(8,128)}), f32[128,64,2,128]{3,0,2,1:T(8,128)}, u32[]{:S(2)}, u32[]{:S(2)}) async-start(f32[128,64,2,128]{3,0,2,1:T(8,128)} %select_bitcast_fusion), calls=%async_computation | async-start | bytes 16777216 | tf_op jit(solution)/shard_map/all_to_all | solution.py:58
  449.9 9.2 %copy-start = (s32[8192,1]{0,1:T(1,128)S(1)}, s32[8192,1]{0,1:T(1,128)}, u32[]{:S(2)}) copy-start(s32[8192,1]{0,1:T(1,128)} %param.17) | copy-start | bytes 98308
  449.9 192.0 %all-to-all-start.1 = ((f32[64,2,128,128]{3,2,1,0:T(8,128)}), f32[64,2,128,128]{3,2,1,0:T(8,128)}, u32[]{:S(2)}, u32[]{:S(2)}) async-start(f32[64,2,128,128]{3,2,1,0:T(8,128)} %broadcast_select_fusion), calls=%async_computation.1 | async-start | bytes 16777216 | tf_op jit(solution)/shard_map/all_to_all | solution.py:83
  458.6 251.4 %reduce-scatter.2.cloned.1.call-start = ((), (), s32[]{:S(2)}) async-start(), calls=%async_computation.7 | async-start | bytes 5242880 | tf_op jit(solution)/shard_map/reduce_scatter | solution.py:94
  712.3 18.0 %all-to-all-start.2 = ((f32[32,4,2048]{2,0,1:T(8,128)}), f32[32,4,2048]{2,0,1:T(8,128)S(1)}, u32[]{:S(2)}, u32[]{:S(2)}) async-start(f32[32,4,2048]{2,0,1:T(8,128)} %bitcast.119), calls=%async_computation.3 | async-start | bytes 2097152 | tf_op jit(solution)/shard_map/all_to_all | solution.py:108
  767.6 18.6 %all-to-all-start.4 = ((f32[32,64,128]{2,0,1:T(8,128)}), f32[32,64,128]{2,0,1:T(8,128)S(1)}, u32[]{:S(2)}, u32[]{:S(2)}) async-start(f32[32,64,128]{2,0,1:T(8,128)} %all_to_all.48), calls=%async_computation.5 | async-start | bytes 2097152 | tf_op jit(solution)/shard_map/all_to_all | solution.py:95
Sparse Core Ops, SparseCore 0:
  9.2 52.6 all-gather.1
  663.2 46.7 reduce-scatter.1
where the time goes:
time: 810 us; the launch traced here: 803 us
  waiting for transfers between devices  480 us (59%)
  local copies, waits for them, and re-layouts  121 us (15%)
  matrix products  100 us (12%)
  blocking collectives  37.3 us (5%)
  starting transfers between devices  32 us (4%)
  other arithmetic  19.6 us (2%)
  between operations  13.7 us (2%)
    all_to_all x1, waiting for transfers between devices, local(): lax.all_to_all(outgoing, 'tile', split_axis=1, concat_axis=1, tiled=True)  182 us
    all_to_all x1, waiting for transfers between devices, local(): lax.all_to_all(outbound, 'tile', split_axis=0, concat_axis=0, tiled=True)  182 us
    dot_general x4, matrix products, one_batch(): jnp.einsum('gpil,gplj->gij', halfway, factors[rights], precision=highest)  47.2 us
    reduce_scatter x1, waiting for transfers between devices, local(): lax.psum_scatter(row_sums, 'aux', scatter_dimension=0, tiled=True)  46.9 us
    all_gather x1, waiting for transfers between devices, local(): row_slab = lax.all_gather(density, 'aux', axis=1, tiled=True)  45.8 us
    dot_general x4, matrix products, one_batch(): jnp.einsum('gpik,kgl->gpil', factors[lefts], dens_block, precision=highest)  44 us
    all_to_all x1, blocking collectives, local(): lax.all_to_all(exchange_rows.reshape(quarter, tiles_all, tile_width), 'ti...  37.3 us
    gather x4, local copies, waits for them, and re-layouts, one_batch(): factors[lefts]  28.4 us
  transfers between devices with their start and end apart: 6, of which 6 were waited for; matrix products, arithmetic and copies ran while one was open for 1% of the time, Pallas kernels for 0%

commit v1 on v0

v1 whole, which is shorter than its diff:
```python
import functools
import jax
import jax.numpy as jnp
from jax import lax
from jax.experimental import pallas as pl
from jax.experimental.pallas import tpu as pltpu
from jax.sharding import PartitionSpec as P

MESH = pl.DeviceIdType.MESH
TILE = 128
CAP = 2
VMEM_BYTES = 56 * 1024 * 1024
STRIDE = 27


def halves(x):
    top = x.astype(jnp.bfloat16)
    rest = (x - top.astype(jnp.float32)).astype(jnp.bfloat16)
    return top, rest


def ranks_of(keys):
    count = keys.shape[-1]
    spot = jnp.arange(count)
    earlier = spot[None, :] < spot[:, None]
    return jnp.sum((keys[..., :, None] == keys[..., None, :]) & earlier, axis=-1).astype(jnp.int32)


def slot_columns(keys, columns, wanted):
    ranking = ranks_of(keys)
    picked = []
    for level in range(CAP):
        chosen = (keys == wanted) & (ranking == level)
        picked.append(jnp.sum(jnp.where(chosen, columns + 1, 0), axis=-1) - 1)
    return jnp.stack(picked, axis=-1)


def density_kernel(n_tile, n_aux, cols_ref, dens_ref, out_ref, slab, outgoing, y_send, y_recv, t_send, t_recv, own_sem):
    me = lax.axis_index("tile")
    aux = lax.axis_index("aux")
    up, down = lax.rem(aux + 1, n_aux), lax.rem(aux + n_aux - 1, n_aux)
    per = dens_ref.shape[1] // TILE
    half = per // 2
    barrier = pltpu.get_barrier_semaphore()

    @pl.loop(1, n_tile)
    def _(s):
        pl.semaphore_signal(barrier, inc=1, device_id={"tile": lax.rem(me + s, n_tile), "aux": aux}, device_id_type=MESH)

    for other in (up, down):
        pl.semaphore_signal(barrier, inc=1, device_id={"tile": me, "aux": other}, device_id_type=MESH)
    pl.semaphore_wait(barrier, n_tile + 1)

    def near(src, dst, index, other):
        return pltpu.make_async_remote_copy(
            src_ref=src, dst_ref=dst, send_sem=y_send.at[index], recv_sem=y_recv.at[index],
            device_id={"tile": me, "aux": other}, device_id_type=MESH)

    for j in range(per):
        slab[aux * per + j] = dens_ref[:, j * TILE:(j + 1) * TILE]

    def part(owner, start, length):
        return slab.at[pl.ds(owner * per + start, length)]

    across = lax.rem(aux + 2, n_aux)
    first_up = near(part(aux, 0, per), part(aux, 0, per), 0, up)
    first_down = near(part(aux, 0, per), part(aux, 0, per), 1, down)
    first_up.start()
    first_down.start()
    near(part(down, 0, per), part(down, 0, per), 0, up).wait_recv()
    second_up = near(part(down, 0, half), part(down, 0, half), 2, up)
    second_up.start()
    near(part(up, 0, per), part(up, 0, per), 1, down).wait_recv()
    second_down = near(part(up, half, half), part(up, half, half), 3, down)
    second_down.start()
    near(part(across, 0, half), part(across, 0, half), 2, up).wait_recv()
    near(part(across, half, half), part(across, half, half), 3, down).wait_recv()

    def pick(dest):
        for level in range(CAP):
            outgoing[dest, level] = slab[cols_ref[dest, level]]

    def far(s):
        offset = lax.rem(s * STRIDE, n_tile)
        dest = lax.rem(me + offset, n_tile)
        return dest, pltpu.make_async_remote_copy(
            src_ref=outgoing.at[dest], dst_ref=out_ref.at[me], send_sem=t_send.at[s], recv_sem=t_recv.at[s],
            device_id={"tile": dest, "aux": aux}, device_id_type=MESH)

    @pl.loop(1, n_tile)
    def _(s):
        dest, copy = far(s)
        pick(dest)
        copy.start()

    pick(me)
    own = pltpu.make_async_copy(outgoing.at[me], out_ref.at[me], own_sem)
    own.start()

    @pl.loop(1, n_tile)
    def _(s):
        offset = lax.rem(s * STRIDE, n_tile)
        source = lax.rem(me + n_tile - offset, n_tile)
        pltpu.make_async_remote_copy(
            src_ref=outgoing.at[me], dst_ref=out_ref.at[source], send_sem=t_send.at[s], recv_sem=t_recv.at[s],
            device_id={"tile": source, "aux": aux}, device_id_type=MESH).wait_recv()

    @pl.loop(1, n_tile)
    def _(s):
        far(s)[1].wait_send()

    own.wait()
    for copy in (first_up, first_down, second_up, second_down):
        copy.wait_send()


def fetch_density(density, cols, n_tile, n_aux):
    return pl.pallas_call(
        functools.partial(density_kernel, n_tile, n_aux),
        out_shape=jax.ShapeDtypeStruct((n_tile, CAP, TILE, TILE), jnp.float32),
        in_specs=[pl.BlockSpec(memory_space=pltpu.SMEM), pl.BlockSpec(memory_space=pltpu.VMEM)],
        out_specs=pl.BlockSpec(memory_space=pl.ANY),
        scratch_shapes=[
            pltpu.VMEM((n_tile, TILE, TILE), jnp.float32),
            pltpu.VMEM((n_tile, CAP, TILE, TILE), jnp.float32),
            pltpu.SemaphoreType.DMA((4,)),
            pltpu.SemaphoreType.DMA((4,)),
            pltpu.SemaphoreType.DMA((n_tile,)),
            pltpu.SemaphoreType.DMA((n_tile,)),
            pltpu.SemaphoreType.DMA,
        ],
        compiler_params=pltpu.CompilerParams(collective_id=0, has_side_effects=True, vmem_limit_bytes=VMEM_BYTES),
        name="fetch_density",
    )(cols, density)


def task_kernel(pair_count, table, dens_ref, fact_ref, out_ref, split):
    q = pl.program_id(0)

    @pl.when(q == 0)
    def _():
        @pl.loop(0, fact_ref.shape[0])
        def _(slot):
            @pl.loop(0, pair_count)
            def _(p):
                rows = pl.ds(pl.multiple_of(p * 2 * TILE, 2 * TILE), 2 * TILE)
                top, rest = halves(fact_ref[slot, rows, :])
                split[slot, rows, 0:TILE] = top
                split[slot, rows, TILE:2 * TILE] = rest

    left, right = table[1, q], table[2, q]
    top, rest = halves(dens_ref[0])
    row = jnp.concatenate([top, rest], axis=1)
    weights = jnp.concatenate([row, row], axis=0)
    total = jnp.zeros((2 * TILE, 2 * TILE), jnp.float32)
    for p in range(pair_count):
        rows = slice(p * 2 * TILE, (p + 1) * 2 * TILE)
        wide = jnp.dot(split[left, rows, :], weights, preferred_element_type=jnp.float32)
        top, rest = halves(wide[:, :TILE] + wide[:, TILE:])
        lhs = jnp.concatenate(
            [jnp.concatenate([top[:TILE], top[TILE:]], axis=1), jnp.concatenate([rest[:TILE], rest[TILE:]], axis=1)], axis=0)
        total = total + jnp.dot(lhs, split[right, rows, :], preferred_element_type=jnp.float32)
    tall = total[:, :TILE] + total[:, TILE:]
    out_ref[0] = tall[:TILE] + tall[TILE:]


def run_tasks(table, incoming, factors, slots):
    slot_count, aux_funcs = factors.shape[:2]
    flat = factors.reshape(slot_count, aux_funcs * TILE, TILE)
    task_count = table.shape[1]
    return pl.pallas_call(
        functools.partial(task_kernel, aux_funcs // 2),
        out_shape=jax.ShapeDtypeStruct((slots, TILE, TILE), jnp.float32),
        grid_spec=pltpu.PrefetchScalarGridSpec(
            num_scalar_prefetch=1,
            grid=(task_count,),
            in_specs=[
                pl.BlockSpec((1, TILE, TILE), lambda q, t: (t[0, q], 0, 0)),
                pl.BlockSpec(flat.shape, lambda q, t: (0, 0, 0), pipeline_mode=pl.Buffered(1)),
            ],
            out_specs=pl.BlockSpec((1, TILE, TILE), lambda q, t: (t[3, q], 0, 0)),
            scratch_shapes=[pltpu.VMEM((slot_count, aux_funcs * TILE, 2 * TILE), jnp.bfloat16)],
        ),
        compiler_params=pltpu.CompilerParams(vmem_limit_bytes=VMEM_BYTES),
        name="run_tasks",
    )(table, incoming, flat)


def return_kernel(n_tile, src_ref, out_ref, t_send, t_recv, own_sem):
    me = lax.axis_index("tile")
    aux = lax.axis_index("aux")
    barrier = pltpu.get_barrier_semaphore()

    @pl.loop(1, n_tile)
    def _(s):
        pl.semaphore_signal(barrier, inc=1, device_id={"tile": lax.rem(me + s, n_tile), "aux": aux}, device_id_type=MESH)

    pl.semaphore_wait(barrier, n_tile - 1)

    def far(s):
        dest = lax.rem(me + lax.rem(s * STRIDE, n_tile), n_tile)
        return pltpu.make_async_remote_copy(
            src_ref=src_ref.at[dest], dst_ref=out_ref.at[me], send_sem=t_send.at[s], recv_sem=t_recv.at[s],
            device_id={"tile": dest, "aux": aux}, device_id_type=MESH)

    @pl.loop(1, n_tile)
    def _(s):
        far(s).start()

    own = pltpu.make_async_copy(src_ref.at[me], out_ref.at[me], own_sem)
    own.start()

    @pl.loop(1, n_tile)
    def _(s):
        source = lax.rem(me + n_tile - lax.rem(s * STRIDE, n_tile), n_tile)
        pltpu.make_async_remote_copy(
            src_ref=src_ref.at[me], dst_ref=out_ref.at[source], send_sem=t_send.at[s], recv_sem=t_recv.at[s],
            device_id={"tile": source, "aux": aux}, device_id_type=MESH).wait_recv()

    @pl.loop(1, n_tile)
    def _(s):
        far(s).wait_send()

    own.wait()


def return_partials(outbound, n_tile):
    return pl.pallas_call(
        functools.partial(return_kernel, n_tile),
        out_shape=jax.ShapeDtypeStruct(outbound.shape, jnp.float32),
        in_specs=[pl.BlockSpec(memory_space=pl.ANY)],
        out_specs=pl.BlockSpec(memory_space=pl.ANY),
        scratch_shapes=[
            pltpu.SemaphoreType.DMA((n_tile,)),
            pltpu.SemaphoreType.DMA((n_tile,)),
            pltpu.SemaphoreType.DMA,
        ],
        compiler_params=pltpu.CompilerParams(collective_id=1, has_side_effects=True),
        name="return_partials",
    )(outbound)


def sum_kernel(group, cols, tiles_ref, out_ref):
    step = pl.program_id(0)

    @pl.when(step == 0)
    def _():
        @pl.loop(0, out_ref.shape[0])
        def _(b):
            out_ref[b] = jnp.zeros((TILE, TILE), jnp.float32)

    for i in range(group):
        col = cols[step * group + i]

        @pl.when(col >= 0)
        def _():
            out_ref[col] = out_ref[col] + tiles_ref[i]


def sum_rows(cols, arrived, n_tile):
    group = 16
    count = arrived.shape[0]
    return pl.pallas_call(
        functools.partial(sum_kernel, group),
        out_shape=jax.ShapeDtypeStruct((n_tile, TILE, TILE), jnp.float32),
        grid_spec=pltpu.PrefetchScalarGridSpec(
            num_scalar_prefetch=1,
            grid=(count // group,),
            in_specs=[pl.BlockSpec((group, TILE, TILE), lambda s, t: (s, 0, 0))],
            out_specs=pl.BlockSpec((n_tile, TILE, TILE), lambda s, t: (0, 0, 0)),
        ),
        compiler_params=pltpu.CompilerParams(vmem_limit_bytes=VMEM_BYTES),
        name="sum_rows",
    )(cols, arrived)


def mirror_kernel(n_tile, n_aux, rows_ref, own_ref, mirror_ref, half_up, half_down, full_up, full_down, outgoing,
                  summed, y_send, y_recv, m_send, m_recv, out_sem):
    me = lax.axis_index("tile")
    aux = lax.axis_index("aux")
    up, down = lax.rem(aux + 1, n_aux), lax.rem(aux + n_aux - 1, n_aux)
    across = lax.rem(aux + 2, n_aux)
    per = n_tile // n_aux
    half = per // 2
    block = me // per
    slot = lax.rem(me, per)
    alike = block == aux
    barrier = pltpu.get_barrier_semaphore()
    for other in (up, down):
        pl.semaphore_signal(barrier, inc=1, device_id={"tile": me, "aux": other}, device_id_type=MESH)

    @pl.loop(0, per)
    def _(j):
        @pl.when(jnp.logical_not(alike & (j == slot)))
        def _():
            pl.semaphore_signal(barrier, inc=1, device_id={"tile": aux * per + j, "aux": block}, device_id_type=MESH)

    pl.semaphore_wait(barrier, jnp.where(alike, per + 1, per + 2))

    def near(src, dst, index, other):
        return pltpu.make_async_remote_copy(
            src_ref=src, dst_ref=dst, send_sem=y_send.at[index], recv_sem=y_recv.at[index],
            device_id={"tile": me, "aux": other}, device_id_type=MESH)

    first_up = near(rows_ref.at[pl.ds(across * per, half)], half_up, 0, up)
    first_down = near(rows_ref.at[pl.ds(across * per + half, half)], half_down, 1, down)
    first_up.start()
    first_down.start()

    @pl.loop(0, per)
    def _(j):
        outgoing[0, j] = rows_ref[up * per + j]
        outgoing[1, j] = rows_ref[down * per + j]

    first_up.wait_recv()

    @pl.loop(0, half)
    def _(j):
        outgoing[0, j] = outgoing[0, j] + half_up[j]

    second_up = near(outgoing.at[0], full_up, 2, up)
    second_up.start()
    first_down.wait_recv()

    @pl.loop(0, half)
    def _(j):
        outgoing[1, half + j] = outgoing[1, half + j] + half_down[j]

    second_down = near(outgoing.at[1], full_down, 3, down)
    second_down.start()
    second_up.wait_recv()
    second_down.wait_recv()

    def send(j):
        return pltpu.make_async_remote_copy(
            src_ref=summed.at[j], dst_ref=mirror_ref.at[slot], send_sem=m_send.at[j], recv_sem=m_recv.at[slot],
            device_id={"tile": aux * per + j, "aux": block}, device_id_type=MESH)

    def keep(j):
        return pltpu.make_async_copy(summed.at[j], mirror_ref.at[j], m_send.at[j])

    @pl.loop(0, per)
    def _(j):
        summed[j] = rows_ref[aux * per + j] + (full_up[j] + full_down[j])
        mine = alike & (j == slot)

        @pl.when(jnp.logical_not(mine))
        def _():
            send(j).start()

        @pl.when(mine)
        def _():
            keep(j).start()

    out_copy = pltpu.make_async_copy(summed, own_ref, out_sem)
    out_copy.start()

    @pl.loop(0, per)
    def _(j):
        mine = alike & (j == slot)

        @pl.when(jnp.logical_not(mine))
        def _():
            pltpu.make_async_remote_copy(
                src_ref=summed.at[j], dst_ref=mirror_ref.at[j], send_sem=m_send.at[j], recv_sem=m_recv.at[j],
                device_id={"tile": aux * per + j, "aux": block}, device_id_type=MESH).wait_recv()
            send(j).wait_send()

        @pl.when(mine)
        def _():
            keep(j).wait()

    out_copy.wait()
    for copy in (first_up, first_down, second_up, second_down):
        copy.wait_send()


def exchange_mirror(rows, n_tile, n_aux):
    per = n_tile // n_aux
    tiles = lambda *lead: pltpu.VMEM(lead + (TILE, TILE), jnp.float32)
    shape = jax.ShapeDtypeStruct((per, TILE, TILE), jnp.float32)
    return pl.pallas_call(
        functools.partial(mirror_kernel, n_tile, n_aux),
        out_shape=(shape, shape),
        in_specs=[pl.BlockSpec(memory_space=pltpu.VMEM)],
        out_specs=(pl.BlockSpec(memory_space=pl.ANY), pl.BlockSpec(memory_space=pl.ANY)),
        scratch_shapes=[
            tiles(per // 2), tiles(per // 2), tiles(per), tiles(per), tiles(2, per), tiles(per),
            pltpu.SemaphoreType.DMA((4,)),
            pltpu.SemaphoreType.DMA((4,)),
            pltpu.SemaphoreType.DMA((per,)),
            pltpu.SemaphoreType.DMA((per,)),
            pltpu.SemaphoreType.DMA,
        ],
        compiler_params=pltpu.CompilerParams(collective_id=2, has_side_effects=True, vmem_limit_bytes=VMEM_BYTES),
        name="exchange_mirror",
    )(rows)


def finish_kernel(place, own_ref, mirror_ref, left_ref, right_ref, out_ref):
    symmetric = own_ref[0] + jnp.transpose(mirror_ref[0])
    dims = (((0,), (0,)), ((), ()))
    leftward = lax.dot_general(left_ref[...], symmetric, dims, precision=lax.Precision.HIGHEST,
                               preferred_element_type=jnp.float32)
    out_ref[...] = jnp.dot(leftward, right_ref[...], precision=lax.Precision.HIGHEST,
                           preferred_element_type=jnp.float32)


def finish(place, own, mirror, orthogonalizers):
    per = own.shape[0]
    tile = pl.BlockSpec((1, TILE, TILE), lambda j, t: (j, 0, 0))
    return pl.pallas_call(
        finish_kernel,
        out_shape=jax.ShapeDtypeStruct((TILE, per * TILE), jnp.float32),
        grid_spec=pltpu.PrefetchScalarGridSpec(
            num_scalar_prefetch=1,
            grid=(per,),
            in_specs=[
                tile, tile,
                pl.BlockSpec((TILE, TILE), lambda j, t: (t[0], 0)),
                pl.BlockSpec((TILE, TILE), lambda j, t: (t[1] * per + j, 0)),
            ],
            out_specs=pl.BlockSpec((TILE, TILE), lambda j, t: (0, j)),
        ),
        name="finish",
    )(place, own, mirror, orthogonalizers, orthogonalizers)


def local(density, factors, orthogonalizers, slot_pairs, density_source, density_column, target_row, target_column):
    n_tile, n_aux = lax.axis_size("tile"), lax.axis_size("aux")
    me, aux = lax.axis_index("tile"), lax.axis_index("aux")
    tasks = slot_pairs.shape[0]

    def group(rows):
        grid = rows.reshape(n_tile, n_aux, tasks)
        return lax.dynamic_index_in_dim(grid, aux, 1, False)

    sources, columns = group(density_source), group(density_column)
    targets, target_cols = group(target_row), group(target_column)
    own_source = lax.dynamic_index_in_dim(sources, me, 0, False)
    own_target = lax.dynamic_index_in_dim(targets, me, 0, False)
    send_cols = slot_columns(sources, columns, me)
    sum_cols = slot_columns(targets, target_cols, me).reshape(-1)
    table = jnp.stack([
        own_source * CAP + ranks_of(own_source),
        slot_pairs[:, 0],
        slot_pairs[:, 1],
        own_target * CAP + ranks_of(own_target),
    ])
    slots = n_tile * CAP
    incoming = fetch_density(density, jnp.maximum(send_cols, 0), n_tile, n_aux)
    outbound = run_tasks(table, incoming.reshape(slots, TILE, TILE), factors, slots)
    arrived = return_partials(outbound.reshape(n_tile, CAP, TILE, TILE), n_tile)
    rows = sum_rows(sum_cols, arrived.reshape(slots, TILE, TILE), n_tile)
    own, mirror = exchange_mirror(rows, n_tile, n_aux)
    return finish(jnp.stack([me, aux]).astype(jnp.int32), own, mirror, orthogonalizers)


def solution(mesh):
    return jax.shard_map(
        local,
        mesh=mesh,
        in_specs=(
            P("tile", "aux"),
            P(("tile", "aux"), None, None, None),
            P(),
            P(("tile", "aux"), None),
            P(),
            P(),
            P(),
            P(),
        ),
        out_specs=P("tile", "aux"),
        check_vma=False,
    )
```

time: 810 us -> 606 us (0.75)
  Pallas kernels: 0 us -> 592 us
  waiting for transfers between devices: 480 us -> 0 us
  local copies, waits for them, and re-layouts: 121 us -> 3.04 us
  matrix products: 100 us -> 0 us
  blocking collectives: 37.3 us -> 0 us
  starting transfers between devices: 32 us -> 0 us
  between operations: 13.7 us -> 0.18 us
  other arithmetic: 19.6 us -> 8.59 us
    pallas_call x0 -> x6, Pallas kernels: none -> 592 us  [the longest x1 229 us: fetch_density(): pl.pallas_call(functools.partial(density_kernel, n_tile, n_aux), out_shap...]
    all_to_all x4 -> x0, waiting for transfers between devices: 387 us -> none  [the longest x1 182 us: local(): lax.all_to_all(outgoing, 'tile', split_axis=1, concat_axis=1, tiled=True)]
    dot_general x11 -> x0, matrix products: 100 us -> none  [the longest x4 47.2 us: one_batch(): jnp.einsum('gpil,gplj->gij', halfway, factors[rights], precision=highest)]
    gather x14 -> x0, local copies, waits for them, and re-layouts: 83.4 us -> none  [the longest x4 28.4 us: one_batch(): factors[lefts]]
    reduce_scatter x1 -> x0, waiting for transfers between devices: 46.9 us -> none  [local(): lax.psum_scatter(row_sums, 'aux', scatter_dimension=0, tiled=True)]
    all_gather x1 -> x0, waiting for transfers between devices: 45.8 us -> none  [local(): row_slab = lax.all_gather(density, 'aux', axis=1, tiled=True)]
    all_to_all x1 -> x0, blocking collectives: 37.3 us -> none  [local(): lax.all_to_all(exchange_rows.reshape(quarter, tiles_all, tile_width), 'ti...]
    all_to_all x4 -> x0, starting transfers between devices: 31.7 us -> none  [the longest x1 11.1 us: local(): lax.all_to_all(outgoing, 'tile', split_axis=1, concat_axis=1, tiled=True)]
  transfers between devices with their start and end apart: 6 -> 0, of which waited for: 6 -> 0; matrix products, arithmetic and copies ran while one was open for 1% -> 0% of each run, Pallas kernels for 0% -> 0%
where the time goes in v1:
time: 606 us; the launch traced here: 604 us
  Pallas kernels  592 us (98%)
  other arithmetic  8.59 us (1%)
    pallas_call x1, Pallas kernels, fetch_density(): pl.pallas_call(functools.partial(density_kernel, n_tile, n_aux), out_shap...  229 us
    pallas_call x1, Pallas kernels, return_partials(): pl.pallas_call(functools.partial(return_kernel, n_tile), out_shape=jax.Sh...  192 us
    pallas_call x1, Pallas kernels, exchange_mirror(): pl.pallas_call(functools.partial(mirror_kernel, n_tile, n_aux), out_shape...  112 us
    pallas_call x1, Pallas kernels, run_tasks(): pl.pallas_call(functools.partial(task_kernel, aux_funcs // 2), out_shape=...  35.8 us
    pallas_call x1, Pallas kernels, finish(): pl.pallas_call(finish_kernel, out_shape=jax.ShapeDtypeStruct((TILE, per *...  13.8 us

profile of v1, /device:TPU:22, one launch (start us, length us, event | category | flops | bytes accessed | tf_op | source)
XLA Modules:
  0.0 603.8 jit_solution(4227754915330463582)
XLA Ops:
  0.0 0.7 pad_add_fusion.3.place
  0.7 0.8 slice_bitcast_fusion.1
  1.4 0.5 broadcast.109
  1.9 1.5 reduce.14
  3.4 1.5 reduce.15
  4.9 1.5 reduce.12
  6.4 1.5 reduce.13
  7.9 0.1 reshape.131
  8.0 0.2 convert_reduce_fusion.2
  8.2 0.1 copy.29
  8.3 0.1 reshape.134
  8.5 0.2 convert_reduce_fusion.3
  8.7 0.1 copy.32
  8.8 0.6 pad_add_fusion.table
  9.4 0.3 convert_reduce_fusion
  9.7 0.1 reshape.132
  9.9 0.1 copy.36
  10.0 0.1 reshape.135
  10.1 0.1 copy.37
  10.3 0.1 copy.31
  10.4 0.7 reshape.133.cols
  11.1 0.1 copy.34
  11.2 0.6 broadcast_maximum_fusion.cols_ref
  11.8 229.5 %fetch_density.1 = f32[64,2,128,128]{3,2,1,0:T(8,128)} custom-call(s32[64,2]{1,0:T(8,128)} %broadcast_maximum_fusion.cols_ref, f32[128,2048]{1,0:T(8,128)} %dens_ref.1), custom_call_target="tpu_custom_call" | custom-call | tf_op jit(solution)/shard_map/fetch_density/pallas_call | solution.py:118
  241.3 35.8 %run_tasks.1 = f32[128,128,128]{2,1,0:T(8,128)} custom-call(s32[4,32]{1,0:T(4,128)} %pad_add_fusion.table, f32[128,128,128]{2,1,0:T(8,128)} %bitcast.52, f32[6,2048,128]{2,1,0:T(8,128)} %bitcast.55), custom_call_target="tpu_custom_call" | custom-call | tf_op jit(solution)/shard_map/run_tasks/pallas_call | solution.py:171
  277.1 192.2 %return_partials.1 = f32[64,2,128,128]{3,2,1,0:T(8,128)} custom-call(f32[64,2,128,128]{3,2,1,0:T(8,128)} %bitcast.53), custom_call_target="tpu_custom_call" | custom-call | tf_op jit(solution)/shard_map/return_partials/pallas_call | solution.py:228
  469.3 8.7 %sum_rows.1.rows_ref = f32[64,128,128]{2,1,0:T(8,128)} custom-call(s32[128]{0:T(128)} %reshape.133.cols, f32[128,128,128]{2,1,0:T(8,128)} %bitcast.54), custom_call_target="tpu_custom_call" | custom-call | tf_op jit(solution)/shard_map/sum_rows/pallas_call | solution.py:263
  478.0 112.0 %exchange_mirror.1 = (f32[16,128,128]{2,1,0:T(8,128)}, f32[16,128,128]{2,1,0:T(8,128)}) custom-call(f32[64,128,128]{2,1,0:T(8,128)} %sum_rows.1.rows_ref), custom_call_target="tpu_custom_call" | custom-call | tf_op jit(solution)/shard_map/exchange_mirror/pallas_call | solution.py:382
  590.0 13.8 %finish.1 = f32[128,2048]{1,0:T(8,128)} custom-call(s32[2]{0:T(128)} %pad_add_fusion.3.place, f32[16,128,128]{2,1,0:T(8,128)} %get-tuple-element.7.own_ref, f32[16,128,128]{2,1,0:T(8,128)} %get-tuple-element.8.mirror_ref, f32[8192,128]{1,0:T(8,128)} %right_ref.1, f32[8192,128]{1,0:T(8,128)} %right_ref.1), custom_call_target="tpu_custom_call" | custom-call | tf_op jit(solution)/shard_map/finish/pallas_call | solution.py:412
  (15 shorter events, 0.3 us)

commit v2 on v1

v2 whole, which is shorter than its diff:
```python
import functools
import jax
import jax.numpy as jnp
from jax import lax
from jax.experimental import pallas as pl
from jax.experimental.pallas import tpu as pltpu
from jax.sharding import PartitionSpec as P

MESH = pl.DeviceIdType.MESH
TILE = 128
CAP = 2
VMEM_BYTES = 56 * 1024 * 1024
STRIDE = 27
CHUNKS = 4
STRIP = TILE // CHUNKS
AHEAD = 2


def halves(x):
    top = x.astype(jnp.bfloat16)
    rest = (x - top.astype(jnp.float32)).astype(jnp.bfloat16)
    return top, rest


def ranks_of(keys):
    count = keys.shape[-1]
    spot = jnp.arange(count)
    earlier = spot[None, :] < spot[:, None]
    return jnp.sum((keys[..., :, None] == keys[..., None, :]) & earlier, axis=-1).astype(jnp.int32)


def slot_columns(keys, columns, wanted):
    ranking = ranks_of(keys)
    picked = []
    for level in range(CAP):
        chosen = (keys == wanted) & (ranking == level)
        picked.append(jnp.sum(jnp.where(chosen, columns + 1, 0), axis=-1) - 1)
    return jnp.stack(picked, axis=-1)


def density_kernel(n_tile, n_aux, cols_ref, dens_ref, out_ref, *scratch):
    slabs, outgoing = scratch[:CHUNKS], scratch[CHUNKS]
    y_send, y_recv, t_send, t_recv, own_sem = scratch[CHUNKS + 1:]
    me = lax.axis_index("tile")
    aux = lax.axis_index("aux")
    up, down = lax.rem(aux + 1, n_aux), lax.rem(aux + n_aux - 1, n_aux)
    across = lax.rem(aux + 2, n_aux)
    per = dens_ref.shape[1] // TILE
    half = per // 2
    barrier = pltpu.get_barrier_semaphore()

    @pl.loop(1, n_tile)
    def _(s):
        pl.semaphore_signal(barrier, inc=1, device_id={"tile": lax.rem(me + s, n_tile), "aux": aux}, device_id_type=MESH)

    for other in (up, down):
        pl.semaphore_signal(barrier, inc=1, device_id={"tile": me, "aux": other}, device_id_type=MESH)
    for r in range(CHUNKS):
        for j in range(per):
            slabs[r][aux * per + j] = dens_ref[r * STRIP:(r + 1) * STRIP, j * TILE:(j + 1) * TILE]
    pl.semaphore_wait(barrier, n_tile + 1)

    def near(r, owner, start, length, index, other):
        where = slabs[r].at[pl.ds(owner * per + start, length)]
        return pltpu.make_async_remote_copy(
            src_ref=where, dst_ref=where, send_sem=y_send.at[r, index], recv_sem=y_recv.at[r, index],
            device_id={"tile": me, "aux": other}, device_id_type=MESH)

    def far(r, s):
        dest = lax.rem(me + lax.rem(s * STRIDE, n_tile), n_tile)
        return dest, pltpu.make_async_remote_copy(
            src_ref=outgoing.at[r, dest], dst_ref=out_ref.at[me, :, pl.ds(r * STRIP, STRIP)],
            send_sem=t_send.at[r, s], recv_sem=t_recv.at[r, s],
            device_id={"tile": dest, "aux": aux}, device_id_type=MESH)

    def own(r):
        return pltpu.make_async_copy(outgoing.at[r, me], out_ref.at[me, :, pl.ds(r * STRIP, STRIP)], own_sem.at[r])

    def first(r):
        near(r, aux, 0, per, 0, up).start()
        near(r, aux, 0, per, 1, down).start()

    first(0)
    for r in range(CHUNKS):
        if r + 1 < CHUNKS:
            first(r + 1)
        near(r, down, 0, per, 0, up).wait_recv()
        near(r, down, 0, half, 2, up).start()
        near(r, up, 0, per, 1, down).wait_recv()
        near(r, up, half, half, 3, down).start()
        near(r, across, 0, half, 2, up).wait_recv()
        near(r, across, half, half, 3, down).wait_recv()

        def pick(dest):
            for level in range(CAP):
                outgoing[r, dest, level] = slabs[r][cols_ref[dest, level]]

        @pl.loop(1, n_tile)
        def _(s):
            dest, copy = far(r, s)
            pick(dest)
            copy.start()

        pick(me)
        own(r).start()

    for r in range(CHUNKS):
        @pl.loop(1, n_tile)
        def _(s):
            source = lax.rem(me + n_tile - lax.rem(s * STRIDE, n_tile), n_tile)
            pltpu.make_async_remote_copy(
                src_ref=outgoing.at[r, me], dst_ref=out_ref.at[source, :, pl.ds(r * STRIP, STRIP)],
                send_sem=t_send.at[r, s], recv_sem=t_recv.at[r, s],
                device_id={"tile": source, "aux": aux}, device_id_type=MESH).wait_recv()
            far(r, s)[1].wait_send()

        own(r).wait()
        near(r, aux, 0, per, 0, up).wait_send()
        near(r, aux, 0, per, 1, down).wait_send()
        near(r, down, 0, half, 2, up).wait_send()
        near(r, up, half, half, 3, down).wait_send()


def fetch_density(density, cols, n_tile, n_aux):
    return pl.pallas_call(
        functools.partial(density_kernel, n_tile, n_aux),
        out_shape=jax.ShapeDtypeStruct((n_tile, CAP, TILE, TILE), jnp.float32),
        in_specs=[pl.BlockSpec(memory_space=pltpu.SMEM), pl.BlockSpec(memory_space=pltpu.VMEM)],
        out_specs=pl.BlockSpec(memory_space=pl.ANY),
        scratch_shapes=[pltpu.VMEM((n_tile, STRIP, TILE), jnp.float32)] * CHUNKS + [
            pltpu.VMEM((CHUNKS, n_tile, CAP, STRIP, TILE), jnp.float32),
            pltpu.SemaphoreType.DMA((CHUNKS, 4)),
            pltpu.SemaphoreType.DMA((CHUNKS, 4)),
            pltpu.SemaphoreType.DMA((CHUNKS, n_tile)),
            pltpu.SemaphoreType.DMA((CHUNKS, n_tile)),
            pltpu.SemaphoreType.DMA((CHUNKS,)),
        ],
        compiler_params=pltpu.CompilerParams(collective_id=0, has_side_effects=True, vmem_limit_bytes=VMEM_BYTES),
        name="fetch_density",
    )(cols, density)


def task_kernel(pair_count, table, dens_ref, fact_ref, out_ref, split):
    q = pl.program_id(0)

    @pl.when(q == 0)
    def _():
        @pl.loop(0, fact_ref.shape[0])
        def _(slot):
            @pl.loop(0, pair_count)
            def _(p):
                rows = pl.ds(pl.multiple_of(p * 2 * TILE, 2 * TILE), 2 * TILE)
                top, rest = halves(fact_ref[slot, rows, :])
                split[slot, rows, 0:TILE] = top
                split[slot, rows, TILE:2 * TILE] = rest

    left, right = table[1, q], table[2, q]
    top, rest = halves(dens_ref[0])
    row = jnp.concatenate([top, rest], axis=1)
    weights = jnp.concatenate([row, row], axis=0)
    total = jnp.zeros((2 * TILE, 2 * TILE), jnp.float32)
    for p in range(pair_count):
        rows = slice(p * 2 * TILE, (p + 1) * 2 * TILE)
        wide = jnp.dot(split[left, rows, :], weights, preferred_element_type=jnp.float32)
        top, rest = halves(wide[:, :TILE] + wide[:, TILE:])
        lhs = jnp.concatenate(
            [jnp.concatenate([top[:TILE], top[TILE:]], axis=1), jnp.concatenate([rest[:TILE], rest[TILE:]], axis=1)], axis=0)
        total = total + jnp.dot(lhs, split[right, rows, :], preferred_element_type=jnp.float32)
    tall = total[:, :TILE] + total[:, TILE:]
    out_ref[0] = tall[:TILE] + tall[TILE:]


def run_tasks(table, incoming, factors, slots):
    slot_count, aux_funcs = factors.shape[:2]
    flat = factors.reshape(slot_count, aux_funcs * TILE, TILE)
    task_count = table.shape[1]
    return pl.pallas_call(
        functools.partial(task_kernel, aux_funcs // 2),
        out_shape=jax.ShapeDtypeStruct((slots, TILE, TILE), jnp.float32),
        grid_spec=pltpu.PrefetchScalarGridSpec(
            num_scalar_prefetch=1,
            grid=(task_count,),
            in_specs=[
                pl.BlockSpec((1, TILE, TILE), lambda q, t: (t[0, q], 0, 0)),
                pl.BlockSpec(flat.shape, lambda q, t: (0, 0, 0), pipeline_mode=pl.Buffered(1)),
            ],
            out_specs=pl.BlockSpec((1, TILE, TILE), lambda q, t: (t[3, q], 0, 0)),
            scratch_shapes=[pltpu.VMEM((slot_count, aux_funcs * TILE, 2 * TILE), jnp.bfloat16)],
        ),
        compiler_params=pltpu.CompilerParams(vmem_limit_bytes=VMEM_BYTES),
        name="run_tasks",
    )(table, incoming, flat)


def return_kernel(n_tile, n_aux, order_ref, src_ref, own_ref, mirror_ref, *scratch):
    arrived = scratch[:CHUNKS]
    (running, rows, half_up, half_down, full_up, full_down, outgoing, summed,
     t_send, t_recv, y_send, y_recv, m_send, m_recv, own_sem, out_sem) = scratch[CHUNKS:]
    me = lax.axis_index("tile")
    aux = lax.axis_index("aux")
    up, down = lax.rem(aux + 1, n_aux), lax.rem(aux + n_aux - 1, n_aux)
    across = lax.rem(aux + 2, n_aux)
    per = n_tile // n_aux
    half = per // 2
    block = me // per
    slot = lax.rem(me, per)
    alike = block == aux
    slots = n_tile * CAP
    barrier = pltpu.get_barrier_semaphore()

    @pl.loop(1, n_tile)
    def _(s):
        pl.semaphore_signal(barrier, inc=1, device_id={"tile": lax.rem(me + s, n_tile), "aux": aux}, device_id_type=MESH)

    for other in (up, down):
        pl.semaphore_signal(barrier, inc=1, device_id={"tile": me, "aux": other}, device_id_type=MESH)

    @pl.loop(0, per)
    def _(j):
        @pl.when(jnp.logical_not(alike & (j == slot)))
        def _():
            pl.semaphore_signal(barrier, inc=1, device_id={"tile": aux * per + j, "aux": block}, device_id_type=MESH)

    pl.semaphore_wait(barrier, n_tile + jnp.where(alike, per, per + 1))

    def far(r, s):
        dest = lax.rem(me + lax.rem(s * STRIDE, n_tile), n_tile)
        return pltpu.make_async_remote_copy(
            src_ref=src_ref.at[dest, :, pl.ds(r * STRIP, STRIP)], dst_ref=arrived[r].at[pl.ds(me * CAP, CAP)],
            send_sem=t_send.at[r, s], recv_sem=t_recv.at[r, s],
            device_id={"tile": dest, "aux": aux}, device_id_type=MESH)

    def own(r):
        return pltpu.make_async_copy(
            src_ref.at[me, :, pl.ds(r * STRIP, STRIP)], arrived[r].at[pl.ds(me * CAP, CAP)], own_sem.at[r])

    def begin(r):
        @pl.loop(1, n_tile)
        def _(s):
            far(r, s).start()

        own(r).start()

    def near(src, dst, r, index, other):
        return pltpu.make_async_remote_copy(
            src_ref=src, dst_ref=dst, send_sem=y_send.at[r, index], recv_sem=y_recv.at[r, index],
            device_id={"tile": me, "aux": other}, device_id_type=MESH)

    def steps(r):
        return (
            near(rows.at[r, pl.ds(across * per, half)], half_up.at[r], r, 0, up),
            near(rows.at[r, pl.ds(across * per + half, half)], half_down.at[r], r, 1, down),
            near(outgoing.at[r, 0], full_up.at[r], r, 2, up),
            near(outgoing.at[r, 1], full_down.at[r], r, 3, down),
        )

    def send(r, j):
        return pltpu.make_async_remote_copy(
            src_ref=summed.at[r, j], dst_ref=mirror_ref.at[slot, pl.ds(r * STRIP, STRIP)],
            send_sem=m_send.at[r, j], recv_sem=m_recv.at[r, slot],
            device_id={"tile": aux * per + j, "aux": block}, device_id_type=MESH)

    def keep(r, j):
        return pltpu.make_async_copy(summed.at[r, j], mirror_ref.at[j, pl.ds(r * STRIP, STRIP)], m_send.at[r, j])

    def settle(r):
        return pltpu.make_async_copy(summed.at[r], own_ref.at[:, pl.ds(r * STRIP, STRIP)], out_sem.at[r])

    for r in range(AHEAD):
        begin(r)
    for r in range(CHUNKS):
        @pl.loop(1, n_tile)
        def _(s):
            source = lax.rem(me + n_tile - lax.rem(s * STRIDE, n_tile), n_tile)
            pltpu.make_async_remote_copy(
                src_ref=src_ref.at[me, :, pl.ds(r * STRIP, STRIP)], dst_ref=arrived[r].at[pl.ds(source * CAP, CAP)],
                send_sem=t_send.at[r, s], recv_sem=t_recv.at[r, s],
                device_id={"tile": source, "aux": aux}, device_id_type=MESH).wait_recv()

        own(r).wait()

        def add(i, carry):
            for u in range(4):
                k = i * 4 + u
                carry = jnp.where(order_ref[1, k] > 0, 0.0, carry) + arrived[r][order_ref[0, k]]
                running[k] = carry
            return carry

        lax.fori_loop(0, slots // 4, add, jnp.zeros((STRIP, TILE), jnp.float32))

        @pl.loop(0, n_tile)
        def _(b):
            rows[r, b] = jnp.where(order_ref[3, b] > 0, running[order_ref[2, b]], 0.0)

        first_up, first_down, second_up, second_down = steps(r)
        first_up.start()
        first_down.start()
        if r + AHEAD < CHUNKS:
            begin(r + AHEAD)

        @pl.loop(0, half)
        def _(j):
            outgoing[r, 0, half + j] = rows[r, up * per + half + j]
            outgoing[r, 1, j] = rows[r, down * per + j]

        first_up.wait_recv()

        @pl.loop(0, half)
        def _(j):
            outgoing[r, 0, j] = rows[r, up * per + j] + half_up[r, j]

        second_up.start()
        first_down.wait_recv()

        @pl.loop(0, half)
        def _(j):
            outgoing[r, 1, half + j] = rows[r, down * per + half + j] + half_down[r, j]

        second_down.start()
        second_up.wait_recv()
        second_down.wait_recv()

        @pl.loop(0, per)
        def _(j):
            summed[r, j] = rows[r, aux * per + j] + (full_up[r, j] + full_down[r, j])
            mine = alike & (j == slot)

            @pl.when(jnp.logical_not(mine))
            def _():
                send(r, j).start()

            @pl.when(mine)
            def _():
                keep(r, j).start()

        settle(r).start()

    for r in range(CHUNKS):
        @pl.loop(1, n_tile)
        def _(s):
            far(r, s).wait_send()

        @pl.loop(0, per)
        def _(j):
            mine = alike & (j == slot)

            @pl.when(jnp.logical_not(mine))
            def _():
                pltpu.make_async_remote_copy(
                    src_ref=summed.at[r, j], dst_ref=mirror_ref.at[j, pl.ds(r * STRIP, STRIP)],
                    send_sem=m_send.at[r, j], recv_sem=m_recv.at[r, j],
                    device_id={"tile": aux * per + j, "aux": block}, device_id_type=MESH).wait_recv()
                send(r, j).wait_send()

            @pl.when(mine)
            def _():
                keep(r, j).wait()

        settle(r).wait()
        for copy in steps(r):
            copy.wait_send()


def return_partials(order, outbound, n_tile, n_aux):
    per = n_tile // n_aux
    strips = lambda *lead: pltpu.VMEM(lead + (STRIP, TILE), jnp.float32)
    shape = jax.ShapeDtypeStruct((per, TILE, TILE), jnp.float32)
    return pl.pallas_call(
        functools.partial(return_kernel, n_tile, n_aux),
        out_shape=(shape, shape),
        in_specs=[pl.BlockSpec(memory_space=pltpu.SMEM), pl.BlockSpec(memory_space=pl.ANY)],
        out_specs=(pl.BlockSpec(memory_space=pl.ANY), pl.BlockSpec(memory_space=pl.ANY)),
        scratch_shapes=[strips(n_tile * CAP)] * CHUNKS + [
            strips(n_tile * CAP), strips(CHUNKS, n_tile),
            strips(CHUNKS, per // 2), strips(CHUNKS, per // 2), strips(CHUNKS, per), strips(CHUNKS, per),
            strips(CHUNKS, 2, per), strips(CHUNKS, per),
            pltpu.SemaphoreType.DMA((CHUNKS, n_tile)),
            pltpu.SemaphoreType.DMA((CHUNKS, n_tile)),
            pltpu.SemaphoreType.DMA((CHUNKS, 4)),
            pltpu.SemaphoreType.DMA((CHUNKS, 4)),
            pltpu.SemaphoreType.DMA((CHUNKS, per)),
            pltpu.SemaphoreType.DMA((CHUNKS, per)),
            pltpu.SemaphoreType.DMA((CHUNKS,)),
            pltpu.SemaphoreType.DMA((CHUNKS,)),
        ],
        compiler_params=pltpu.CompilerParams(collective_id=1, has_side_effects=True, vmem_limit_bytes=VMEM_BYTES),
        name="return_partials",
    )(order, outbound)


def stacked(x, axis):
    return jnp.concatenate(halves(x), axis=axis)


def folded(x):
    tall = x[:, :TILE] + x[:, TILE:]
    return tall[:TILE] + tall[TILE:]


def finish_kernel(group, place, own_ref, mirror_ref, left_ref, right_ref, out_ref):
    left = stacked(jnp.transpose(left_ref[...]), 0)
    for i in range(group):
        symmetric = own_ref[i] + jnp.transpose(mirror_ref[i])
        leftward = folded(jnp.dot(left, stacked(symmetric, 1), preferred_element_type=jnp.float32))
        right = stacked(right_ref[i * TILE:(i + 1) * TILE, :], 1)
        out_ref[:, i * TILE:(i + 1) * TILE] = folded(
            jnp.dot(stacked(leftward, 0), right, preferred_element_type=jnp.float32))


def finish(place, own, mirror, orthogonalizers):
    per = own.shape[0]
    group = 4
    steps = per // group
    tile = pl.BlockSpec((group, TILE, TILE), lambda j, t: (j, 0, 0))
    return pl.pallas_call(
        functools.partial(finish_kernel, group),
        out_shape=jax.ShapeDtypeStruct((TILE, per * TILE), jnp.float32),
        grid_spec=pltpu.PrefetchScalarGridSpec(
            num_scalar_prefetch=1,
            grid=(steps,),
            in_specs=[
                tile, tile,
                pl.BlockSpec((TILE, TILE), lambda j, t: (t[0], 0)),
                pl.BlockSpec((group * TILE, TILE), lambda j, t: (t[1] * steps + j, 0)),
            ],
            out_specs=pl.BlockSpec((TILE, group * TILE), lambda j, t: (0, j)),
        ),
        name="finish",
    )(place, own, mirror, orthogonalizers, orthogonalizers)


def column_order(cols, n_tile):
    count = cols.shape[0]
    spot = jnp.arange(count, dtype=jnp.int32)
    key = jnp.where(cols < 0, n_tile, cols)
    before = (key[None, :] < key[:, None]) | ((key[None, :] == key[:, None]) & (spot[None, :] < spot[:, None]))
    place = jnp.sum(before, axis=1)
    at = place[None, :] == spot[:, None]
    order = jnp.sum(jnp.where(at, spot[None, :], 0), axis=1)
    starts = jnp.any(at & (~jnp.any(before & (key[None, :] == key[:, None]), axis=1))[None, :], axis=1)
    ends = jnp.sum(key[None, :] <= spot[:, None], axis=1) - 1
    held = jnp.any(key[None, :] == spot[:, None], axis=1) & (spot < n_tile)
    return jnp.stack([order, starts.astype(jnp.int32), jnp.maximum(ends, 0), held.astype(jnp.int32)]).astype(jnp.int32)


def local(density, factors, orthogonalizers, slot_pairs, density_source, density_column, target_row, target_column):
    n_tile, n_aux = lax.axis_size("tile"), lax.axis_size("aux")
    me, aux = lax.axis_index("tile"), lax.axis_index("aux")
    tasks = slot_pairs.shape[0]

    def group(rows):
        grid = rows.reshape(n_tile, n_aux, tasks)
        return lax.dynamic_index_in_dim(grid, aux, 1, False)

    sources, columns = group(density_source), group(density_column)
    targets, target_cols = group(target_row), group(target_column)
    own_source = lax.dynamic_index_in_dim(sources, me, 0, False)
    own_target = lax.dynamic_index_in_dim(targets, me, 0, False)
    send_cols = slot_columns(sources, columns, me)
    sum_cols = slot_columns(targets, target_cols, me).reshape(-1)
    table = jnp.stack([
        own_source * CAP + ranks_of(own_source),
        slot_pairs[:, 0],
        slot_pairs[:, 1],
        own_target * CAP + ranks_of(own_target),
    ])
    slots = n_tile * CAP
    incoming = fetch_density(density, jnp.maximum(send_cols, 0), n_tile, n_aux)
    outbound = run_tasks(table, incoming.reshape(slots, TILE, TILE), factors, slots)
    own, mirror = return_partials(
        column_order(sum_cols, n_tile), outbound.reshape(n_tile, CAP, TILE, TILE), n_tile, n_aux)
    return finish(jnp.stack([me, aux]).astype(jnp.int32), own, mirror, orthogonalizers)


def solution(mesh):
    return jax.shard_map(
        local,
        mesh=mesh,
        in_specs=(
            P("tile", "aux"),
            P(("tile", "aux"), None, None, None),
            P(),
            P(("tile", "aux"), None),
            P(),
            P(),
            P(),
            P(),
        ),
        out_specs=P("tile", "aux"),
        check_vma=False,
    )
```

time: 606 us -> 512 us (0.84)
  Pallas kernels: 592 us -> 494 us
    pallas_call x4 -> x2, Pallas kernels: 327 us -> 246 us  [the longest x1 240 us: return_partials(): pl.pallas_call(functools.partial(return_kernel, n_tile, n_aux), out_shape...]
    pallas_call x1, Pallas kernels: 229 us -> 213 us  [fetch_density(): pl.pallas_call(functools.partial(density_kernel, n_tile, n_aux), out_shap...]
where the time goes in v2:
time: 512 us; the launch traced here: 506 us
  Pallas kernels  494 us (96%)
  other arithmetic  9.78 us (2%)
    pallas_call x1, Pallas kernels, return_partials(): pl.pallas_call(functools.partial(return_kernel, n_tile, n_aux), out_shape...  240 us
    pallas_call x1, Pallas kernels, fetch_density(): pl.pallas_call(functools.partial(density_kernel, n_tile, n_aux), out_shap...  213 us
    pallas_call x1, Pallas kernels, run_tasks(): pl.pallas_call(functools.partial(task_kernel, aux_funcs // 2), out_shape=...  35.8 us

profile of v2, /device:TPU:22, one launch (start us, length us, event | category | flops | bytes accessed | tf_op | source)
XLA Modules:
  0.0 506.2 jit_solution(18154590025030779184)
XLA Ops:
  0.0 0.0 copy-start
  0.0 0.5 broadcast.162
  0.5 1.5 reduce.12
  2.0 0.1 reshape.190
  2.2 0.1 copy.29
  2.2 1.5 reduce.14
  3.7 0.1 reshape.193
  3.9 0.1 copy.32
  4.0 0.3 convert_reduce_fusion
  4.3 1.5 reduce.15
  5.8 0.1 reshape.194
  5.9 0.1 copy.37
  6.1 1.5 reduce.13
  7.5 0.1 reshape.191
  7.7 0.1 copy.36
  7.9 0.1 copy.34
  8.0 0.6 broadcast_maximum_fusion.cols_ref
  8.6 213.2 %fetch_density.1 = f32[64,2,128,128]{3,2,1,0:T(8,128)} custom-call(s32[64,2]{1,0:T(8,128)} %broadcast_maximum_fusion.cols_ref, f32[128,2048]{1,0:T(8,128)} %dens_ref.1), custom_call_target="tpu_custom_call" | custom-call | tf_op jit(solution)/shard_map/fetch_density/pallas_call | solution.py:125
  221.8 0.2 convert_reduce_fusion.4
  222.0 0.2 convert_reduce_fusion.5
  222.2 0.0 copy-done
  222.2 0.6 pad_add_fusion.1.table
  222.8 35.8 %run_tasks.1 = f32[128,128,128]{2,1,0:T(8,128)} custom-call(s32[4,32]{1,0:T(4,128)} %pad_add_fusion.1.table, f32[128,128,128]{2,1,0:T(8,128)} %bitcast.60, f32[6,2048,128]{2,1,0:T(8,128)} %bitcast.62), custom_call_target="tpu_custom_call" | custom-call | tf_op jit(solution)/shard_map/run_tasks/pallas_call | solution.py:177
  258.6 0.1 copy.31
  258.7 0.1 reshape.192
  258.8 0.2 fusion.4
  259.0 0.2 convert_reduce_fusion.3
  259.2 0.1 fusion.2
  259.4 0.1 select_reduce_fusion
  259.5 0.6 pad_add_fusion.order_ref
  260.1 239.7 %return_partials.1 = (f32[16,128,128]{2,1,0:T(8,128)}, f32[16,128,128]{2,1,0:T(8,128)}) custom-call(s32[4,128]{1,0:T(4,128)} %pad_add_fusion.order_ref, f32[64,2,128,128]{3,2,1,0:T(8,128)} %bitcast.61), custom_call_target="tpu_custom_call" | custom-call | tf_op jit(solution)/shard_map/return_partials/pallas_call | solution.py:368
  499.8 0.6 pad_add_fusion.4.place
  500.4 5.8 %finish.1 = f32[128,2048]{1,0:T(8,128)} custom-call(s32[2]{0:T(128)} %pad_add_fusion.4.place, f32[16,128,128]{2,1,0:T(8,128)} %get-tuple-element.7.own_ref, f32[16,128,128]{2,1,0:T(8,128)} %get-tuple-element.8.mirror_ref, f32[8192,128]{1,0:T(8,128)} %right_ref.1, f32[8192,128]{1,0:T(8,128)} %right_ref.1), custom_call_target="tpu_custom_call" | custom-call | tf_op jit(solution)/shard_map/finish/pallas_call | solution.py:415
  (21 shorter events, 0.3 us)
Async XLA Ops:
  0.0 222.2 %copy-start = (s32[32,2]{0,1:T(2,128)S(1)}, s32[32,2]{0,1:T(2,128)}, u32[]{:S(2)}) copy-start(s32[32,2]{0,1:T(2,128)} %param.11) | copy-start | bytes 772

commit v3 on v2

--- a/solution.py
+++ b/solution.py
@@ -14,6 +14,11 @@
 CHUNKS = 4
 STRIP = TILE // CHUNKS
 AHEAD = 2
+RING = 8
+CORES = 2
+ORDER = 13
+ROWS = (48, 80)
+SPANS = [(sum(ROWS[:r]), n) for r, n in enumerate(ROWS)]
 
 
 def halves(x):
@@ -38,15 +43,54 @@
     return jnp.stack(picked, axis=-1)
 
 
+def spot_of(tile):
+    return tile // (RING * CORES), lax.rem(tile // CORES, RING), lax.rem(tile, CORES)
+
+
+def tile_of(x, z, core):
+    return (x * RING + z) * CORES + core
+
+
+def opposite(tile):
+    x, z, core = spot_of(tile)
+    return tile_of(x, lax.rem(z + RING // 2, RING), core)
+
+
+def reach(turn, core):
+    far = jnp.where(core == 0, 2, RING - 2)
+    return jnp.where(turn == 3, far, jnp.where(turn == 2, RING - 1, turn))
+
+
+def served(tile, k, n_tile):
+    x, z, core = spot_of(tile)
+    across = n_tile // (RING * CORES)
+    to_core = lax.rem(core + lax.rem(k, CORES), CORES)
+    turn = lax.rem(k // CORES, 4)
+    return tile_of(lax.rem(x + k // (4 * CORES), across), lax.rem(z + reach(turn, core), RING), to_core)
+
+
+def holder(tile, k, n_tile):
+    x, z, core = spot_of(tile)
+    across = n_tile // (RING * CORES)
+    from_core = lax.rem(core + CORES - lax.rem(k, CORES), CORES)
+    turn = lax.rem(k // CORES, 4)
+    return tile_of(lax.rem(x + across - k // (4 * CORES), across), lax.rem(z + RING - reach(turn, from_core), RING), from_core)
+
+
 def density_kernel(n_tile, n_aux, cols_ref, dens_ref, out_ref, *scratch):
-    slabs, outgoing = scratch[:CHUNKS], scratch[CHUNKS]
-    y_send, y_recv, t_send, t_recv, own_sem = scratch[CHUNKS + 1:]
+    parts = len(ROWS)
+    slabs, outgoing = scratch[:2 * parts], scratch[2 * parts:4 * parts]
+    y_send, y_recv, z_send, z_recv, t_send, t_recv, own_sem = scratch[4 * parts:]
     me = lax.axis_index("tile")
     aux = lax.axis_index("aux")
+    far_side = opposite(me)
+    homes = [me] * parts + [far_side] * parts
+    spans = SPANS * 2
     up, down = lax.rem(aux + 1, n_aux), lax.rem(aux + n_aux - 1, n_aux)
     across = lax.rem(aux + 2, n_aux)
     per = dens_ref.shape[1] // TILE
     half = per // 2
+    peers = n_tile // 2
     barrier = pltpu.get_barrier_semaphore()
 
     @pl.loop(1, n_tile)
@@ -55,9 +99,9 @@
 
     for other in (up, down):
         pl.semaphore_signal(barrier, inc=1, device_id={"tile": me, "aux": other}, device_id_type=MESH)
-    for r in range(CHUNKS):
+    for r, (start, length) in enumerate(SPANS):
         for j in range(per):
-            slabs[r][aux * per + j] = dens_ref[r * STRIP:(r + 1) * STRIP, j * TILE:(j + 1) * TILE]
+            slabs[r][aux * per + j] = dens_ref[start:start + length, j * TILE:(j + 1) * TILE]
     pl.semaphore_wait(barrier, n_tile + 1)
 
     def near(r, owner, start, length, index, other):
@@ -66,74 +110,114 @@
             src_ref=where, dst_ref=where, send_sem=y_send.at[r, index], recv_sem=y_recv.at[r, index],
             device_id={"tile": me, "aux": other}, device_id_type=MESH)
 
-    def far(r, s):
-        dest = lax.rem(me + lax.rem(s * STRIDE, n_tile), n_tile)
-        return dest, pltpu.make_async_remote_copy(
-            src_ref=outgoing.at[r, dest], dst_ref=out_ref.at[me, :, pl.ds(r * STRIP, STRIP)],
-            send_sem=t_send.at[r, s], recv_sem=t_recv.at[r, s],
-            device_id={"tile": dest, "aux": aux}, device_id_type=MESH)
+    def swap(r):
+        mine = pl.ds(aux * per, per)
+        return pltpu.make_async_remote_copy(
+            src_ref=slabs[r].at[mine], dst_ref=slabs[parts + r].at[mine], send_sem=z_send.at[r], recv_sem=z_recv.at[r],
+            device_id={"tile": far_side, "aux": aux}, device_id_type=MESH)
+
+    def home_rows(tile, r):
+        return out_ref.at[tile, :, pl.ds(*spans[r])]
+
+    def ship(r, k):
+        return pltpu.make_async_remote_copy(
+            src_ref=outgoing[r].at[k], dst_ref=home_rows(homes[r], r),
+            send_sem=t_send.at[r, k], recv_sem=t_recv.at[r, k],
+            device_id={"tile": served(me, k, n_tile), "aux": aux}, device_id_type=MESH)
 
     def own(r):
-        return pltpu.make_async_copy(outgoing.at[r, me], out_ref.at[me, :, pl.ds(r * STRIP, STRIP)], own_sem.at[r])
+        return pltpu.make_async_copy(outgoing[r].at[0], home_rows(homes[r], r), own_sem.at[r])
 
     def first(r):
         near(r, aux, 0, per, 0, up).start()
         near(r, aux, 0, per, 1, down).start()
 
-    first(0)
-    for r in range(CHUNKS):
-        if r + 1 < CHUNKS:
-            first(r + 1)
+    def second(r):
         near(r, down, 0, per, 0, up).wait_recv()
         near(r, down, 0, half, 2, up).start()
         near(r, up, 0, per, 1, down).wait_recv()
         near(r, up, half, half, 3, down).start()
+
+    def gathered(r):
         near(r, across, 0, half, 2, up).wait_recv()
         near(r, across, half, half, 3, down).wait_recv()
 
-        def pick(dest):
+    def send_all(r):
+        base = 0 if r < parts else n_tile
+
+        @pl.loop(0, peers)
+        def _(s):
+            k = lax.rem(s * ORDER, peers)
+            dest = base + served(me, k, n_tile)
             for level in range(CAP):
-                outgoing[r, dest, level] = slabs[r][cols_ref[dest, level]]
-
-        @pl.loop(1, n_tile)
-        def _(s):
-            dest, copy = far(r, s)
-            pick(dest)
-            copy.start()
-
-        pick(me)
+                outgoing[r][k, level] = slabs[r][cols_ref[dest, level]]
+
+            @pl.when(s > 0)
+            def _():
+                ship(r, k).start()
+
         own(r).start()
 
-    for r in range(CHUNKS):
-        @pl.loop(1, n_tile)
-        def _(s):
-            source = lax.rem(me + n_tile - lax.rem(s * STRIDE, n_tile), n_tile)
+    def step_copy(r):
+        swap(r).wait_recv()
+        first(parts + r)
+
+    first(0)
+    swap(0).start()
+    first(1)
+    swap(1).start()
+    second(0)
+    gathered(0)
+    send_all(0)
+    second(1)
+    step_copy(0)
+    gathered(1)
+    second(2)
+    send_all(1)
+    gathered(2)
+    step_copy(1)
+    send_all(2)
+    second(3)
+    gathered(3)
+    send_all(3)
+
+    for r in range(2 * parts):
+        @pl.loop(1, peers)
+        def _(k):
+            source = holder(me, k, n_tile)
+            home = source if r < parts else opposite(source)
             pltpu.make_async_remote_copy(
-                src_ref=outgoing.at[r, me], dst_ref=out_ref.at[source, :, pl.ds(r * STRIP, STRIP)],
-                send_sem=t_send.at[r, s], recv_sem=t_recv.at[r, s],
+                src_ref=outgoing[r].at[k], dst_ref=home_rows(home, r),
+                send_sem=t_send.at[r, k], recv_sem=t_recv.at[r, k],
                 device_id={"tile": source, "aux": aux}, device_id_type=MESH).wait_recv()
-            far(r, s)[1].wait_send()
+            ship(r, k).wait_send()
 
         own(r).wait()
         near(r, aux, 0, per, 0, up).wait_send()
         near(r, aux, 0, per, 1, down).wait_send()
         near(r, down, 0, half, 2, up).wait_send()
         near(r, up, half, half, 3, down).wait_send()
+        if r < parts:
+            swap(r).wait_send()
 
 
 def fetch_density(density, cols, n_tile, n_aux):
+    units = 2 * len(ROWS)
     return pl.pallas_call(
         functools.partial(density_kernel, n_tile, n_aux),
         out_shape=jax.ShapeDtypeStruct((n_tile, CAP, TILE, TILE), jnp.float32),
         in_specs=[pl.BlockSpec(memory_space=pltpu.SMEM), pl.BlockSpec(memory_space=pltpu.VMEM)],
         out_specs=pl.BlockSpec(memory_space=pl.ANY),
-        scratch_shapes=[pltpu.VMEM((n_tile, STRIP, TILE), jnp.float32)] * CHUNKS + [
-            pltpu.VMEM((CHUNKS, n_tile, CAP, STRIP, TILE), jnp.float32),
-            pltpu.SemaphoreType.DMA((CHUNKS, 4)),
-            pltpu.SemaphoreType.DMA((CHUNKS, 4)),
-            pltpu.SemaphoreType.DMA((CHUNKS, n_tile)),
-            pltpu.SemaphoreType.DMA((CHUNKS, n_tile)),
-            pltpu.SemaphoreType.DMA((CHUNKS,)),
+        scratch_shapes=[pltpu.VMEM((n_tile, n, TILE), jnp.float32) for n in ROWS * 2]
+        + [pltpu.VMEM((n_tile // 2, CAP, n, TILE), jnp.float32) for n in ROWS * 2]
+        + [
+            pltpu.SemaphoreType.DMA((units, 4)),
+            pltpu.SemaphoreType.DMA((units, 4)),
+            pltpu.SemaphoreType.DMA((len(ROWS),)),
+            pltpu.SemaphoreType.DMA((len(ROWS),)),
+            pltpu.SemaphoreType.DMA((units, n_tile // 2)),
+            pltpu.SemaphoreType.DMA((units, n_tile // 2)),
+            pltpu.SemaphoreType.DMA((units,)),
         ],
         compiler_params=pltpu.CompilerParams(collective_id=0, has_side_effects=True, vmem_limit_bytes=VMEM_BYTES),
         name="fetch_density",
@@ -456,7 +540,7 @@
     targets, target_cols = group(target_row), group(target_column)
     own_source = lax.dynamic_index_in_dim(sources, me, 0, False)
     own_target = lax.dynamic_index_in_dim(targets, me, 0, False)
-    send_cols = slot_columns(sources, columns, me)
+    send_cols = jnp.concatenate([slot_columns(sources, columns, me), slot_columns(sources, columns, opposite(me))])
     sum_cols = slot_columns(targets, target_cols, me).reshape(-1)
     table = jnp.stack([
         own_source * CAP + ranks_of(own_source),

time: 512 us -> 453 us (0.88)
  Pallas kernels: 494 us -> 438 us
    pallas_call x1, Pallas kernels: 213 us -> 150 us  [fetch_density(): pl.pallas_call(functools.partial(density_kernel, n_tile, n_aux), out_shap...]
    pallas_call x1, Pallas kernels: 240 us -> 246 us  [return_partials(): pl.pallas_call(functools.partial(return_kernel, n_tile, n_aux), out_shape...]
where the time goes in v3:
time: 453 us; the launch traced here: 451 us
  Pallas kernels  438 us (97%)
  other arithmetic  9.88 us (2%)
    pallas_call x1, Pallas kernels, return_partials(): pl.pallas_call(functools.partial(return_kernel, n_tile, n_aux), out_shape...  246 us
    pallas_call x1, Pallas kernels, fetch_density(): pl.pallas_call(functools.partial(density_kernel, n_tile, n_aux), out_shap...  150 us
    pallas_call x1, Pallas kernels, run_tasks(): pl.pallas_call(functools.partial(task_kernel, aux_funcs // 2), out_shape=...  35.8 us

profile of v3, /device:TPU:22, one launch (start us, length us, event | category | flops | bytes accessed | tf_op | source)
XLA Modules:
  0.0 450.9 jit_solution(14056004126066307028)
XLA Ops:
  0.0 0.6 pad_add_fusion.3.place
  0.6 0.8 slice_bitcast_fusion.1
  1.4 0.5 broadcast.191
  1.9 1.5 reduce.14
  3.4 1.5 reduce.15
  4.9 1.5 reduce.12
  6.4 1.5 reduce.13
  7.8 0.1 reshape.208
  8.0 0.2 convert_reduce_fusion.4
  8.2 0.1 reshape.211
  8.3 0.2 convert_reduce_fusion.5
  8.5 0.6 pad_add_fusion.1.table
  9.1 0.1 reshape.209
  9.2 0.1 constant_dynamic-slice_fusion.4
  9.3 0.1 copy.40
  9.4 0.1 copy.33
  9.4 0.1 reshape.212
  9.6 0.1 constant_dynamic-slice_fusion
  9.7 0.1 copy.41
  9.7 0.1 copy.36
  9.8 0.3 convert_reduce_fusion
  10.3 0.1 add_add_fusion
  10.4 0.1 copy.35
  10.5 0.1 reshape.210
  10.6 0.2 convert_reduce_fusion.3
  10.8 0.1 select_reduce_fusion
  10.9 0.2 fusion.4
  11.1 0.1 fusion.2
  11.3 0.6 pad_add_fusion.order_ref
  11.9 0.1 copy.38
  12.0 0.6 broadcast_maximum_fusion.cols_ref
  12.6 150.2 %fetch_density.1 = f32[64,2,128,128]{3,2,1,0:T(8,128)} custom-call(s32[128,2]{1,0:T(8,128)} %broadcast_maximum_fusion.cols_ref, f32[128,2048]{1,0:T(8,128)} %dens_ref.1), custom_call_target="tpu_custom_call" | custom-call | tf_op jit(solution)/shard_map/fetch_density/pallas_call | solution.py:206
  162.9 35.8 %run_tasks.1 = f32[128,128,128]{2,1,0:T(8,128)} custom-call(s32[4,32]{1,0:T(4,128)} %pad_add_fusion.1.table, f32[128,128,128]{2,1,0:T(8,128)} %bitcast.72, f32[6,2048,128]{2,1,0:T(8,128)} %bitcast.73), custom_call_target="tpu_custom_call" | custom-call | tf_op jit(solution)/shard_map/run_tasks/pallas_call | solution.py:261
  198.6 246.5 %return_partials.1 = (f32[16,128,128]{2,1,0:T(8,128)}, f32[16,128,128]{2,1,0:T(8,128)}) custom-call(s32[4,128]{1,0:T(4,128)} %pad_add_fusion.order_ref, f32[64,2,128,128]{3,2,1,0:T(8,128)} %bitcast.71), custom_call_target="tpu_custom_call" | custom-call | tf_op jit(solution)/shard_map/return_partials/pallas_call | solution.py:452
  445.1 5.8 %finish.1 = f32[128,2048]{1,0:T(8,128)} custom-call(s32[2]{0:T(128)} %pad_add_fusion.3.place, f32[16,128,128]{2,1,0:T(8,128)} %get-tuple-element.7.own_ref, f32[16,128,128]{2,1,0:T(8,128)} %get-tuple-element.8.mirror_ref, f32[8192,128]{1,0:T(8,128)} %right_ref.1, f32[8192,128]{1,0:T(8,128)} %right_ref.1), custom_call_target="tpu_custom_call" | custom-call | tf_op jit(solution)/shard_map/finish/pallas_call | solution.py:499
  (20 shorter events, 0.2 us)

commit v4 on v3

--- a/solution.py
+++ b/solution.py
@@ -10,15 +10,13 @@
 TILE = 128
 CAP = 2
 VMEM_BYTES = 56 * 1024 * 1024
-STRIDE = 27
-CHUNKS = 4
-STRIP = TILE // CHUNKS
-AHEAD = 2
 RING = 8
 CORES = 2
 ORDER = 13
 ROWS = (48, 80)
 SPANS = [(sum(ROWS[:r]), n) for r, n in enumerate(ROWS)]
+BACK = (56, 40, 32)
+BACK_SPANS = [(sum(BACK[:r]), n) for r, n in enumerate(BACK)]
 
 
 def halves(x):
@@ -277,19 +275,23 @@
 
 
 def return_kernel(n_tile, n_aux, order_ref, src_ref, own_ref, mirror_ref, *scratch):
-    arrived = scratch[:CHUNKS]
-    (running, rows, half_up, half_down, full_up, full_down, outgoing, summed,
-     t_send, t_recv, y_send, y_recv, m_send, m_recv, own_sem, out_sem) = scratch[CHUNKS:]
+    parts = len(BACK)
+    units = 2 * parts
+    groups = [scratch[i * units:(i + 1) * units] for i in range(8)]
+    arrived, rows, half_up, half_down, full_up, full_down, outgoing, summed = groups
+    swapped = scratch[8 * units:8 * units + parts]
+    (running, t_send, t_recv, y_send, y_recv, m_send, m_recv, z_send, z_recv, own_sem, out_sem) = scratch[8 * units + parts:]
     me = lax.axis_index("tile")
     aux = lax.axis_index("aux")
+    far_side = opposite(me)
     up, down = lax.rem(aux + 1, n_aux), lax.rem(aux + n_aux - 1, n_aux)
     across = lax.rem(aux + 2, n_aux)
     per = n_tile // n_aux
     half = per // 2
+    peers = n_tile // 2
     block = me // per
     slot = lax.rem(me, per)
     alike = block == aux
-    slots = n_tile * CAP
     barrier = pltpu.get_barrier_semaphore()
 
     @pl.loop(1, n_tile)
@@ -307,165 +309,194 @@
 
     pl.semaphore_wait(barrier, n_tile + jnp.where(alike, per, per + 1))
 
-    def far(r, s):
-        dest = lax.rem(me + lax.rem(s * STRIDE, n_tile), n_tile)
+    def span(u):
+        return pl.ds(*BACK_SPANS[u // 2])
+
+    def home_of(tile, u):
+        return opposite(tile) if u % 2 == 0 else tile
+
+    def far(u, k):
+        dest = holder(me, k, n_tile)
         return pltpu.make_async_remote_copy(
-            src_ref=src_ref.at[dest, :, pl.ds(r * STRIP, STRIP)], dst_ref=arrived[r].at[pl.ds(me * CAP, CAP)],
-            send_sem=t_send.at[r, s], recv_sem=t_recv.at[r, s],
+            src_ref=src_ref.at[home_of(dest, u), :, span(u)], dst_ref=arrived[u].at[pl.ds(k * CAP, CAP)],
+            send_sem=t_send.at[u, k], recv_sem=t_recv.at[u, k],
             device_id={"tile": dest, "aux": aux}, device_id_type=MESH)
 
-    def own(r):
-        return pltpu.make_async_copy(
-            src_ref.at[me, :, pl.ds(r * STRIP, STRIP)], arrived[r].at[pl.ds(me * CAP, CAP)], own_sem.at[r])
-
-    def begin(r):
-        @pl.loop(1, n_tile)
+    def own(u):
+        return pltpu.make_async_copy(src_ref.at[home_of(me, u), :, span(u)], arrived[u].at[pl.ds(0, CAP)], own_sem.at[u])
+
+    def begin(u):
+        @pl.loop(1, peers)
         def _(s):
-            far(r, s).start()
-
-        own(r).start()
-
-    def near(src, dst, r, index, other):
+            far(u, lax.rem(s * ORDER, peers)).start()
+
+        own(u).start()
+
+    def near(src, dst, u, index, other):
         return pltpu.make_async_remote_copy(
-            src_ref=src, dst_ref=dst, send_sem=y_send.at[r, index], recv_sem=y_recv.at[r, index],
+            src_ref=src, dst_ref=dst, send_sem=y_send.at[u, index], recv_sem=y_recv.at[u, index],
             device_id={"tile": me, "aux": other}, device_id_type=MESH)
 
-    def steps(r):
+    def steps(u):
         return (
-            near(rows.at[r, pl.ds(across * per, half)], half_up.at[r], r, 0, up),
-            near(rows.at[r, pl.ds(across * per + half, half)], half_down.at[r], r, 1, down),
-            near(outgoing.at[r, 0], full_up.at[r], r, 2, up),
-            near(outgoing.at[r, 1], full_down.at[r], r, 3, down),
+            near(rows[u].at[pl.ds(across * per, half)], half_up[u], u, 0, up),
+            near(rows[u].at[pl.ds(across * per + half, half)], half_down[u], u, 1, down),
+            near(outgoing[u].at[0], full_up[u], u, 2, up),
+            near(outgoing[u].at[1], full_down[u], u, 3, down),
         )
 
-    def send(r, j):
+    def swap(p):
         return pltpu.make_async_remote_copy(
-            src_ref=summed.at[r, j], dst_ref=mirror_ref.at[slot, pl.ds(r * STRIP, STRIP)],
-            send_sem=m_send.at[r, j], recv_sem=m_recv.at[r, slot],
+            src_ref=summed[2 * p], dst_ref=swapped[p], send_sem=z_send.at[p], recv_sem=z_recv.at[p],
+            device_id={"tile": far_side, "aux": aux}, device_id_type=MESH)
+
+    def send(u, j):
+        return pltpu.make_async_remote_copy(
+            src_ref=summed[u].at[j], dst_ref=mirror_ref.at[slot, span(u)],
+            send_sem=m_send.at[u, j], recv_sem=m_recv.at[u, slot],
             device_id={"tile": aux * per + j, "aux": block}, device_id_type=MESH)
 
-    def keep(r, j):
-        return pltpu.make_async_copy(summed.at[r, j], mirror_ref.at[j, pl.ds(r * STRIP, STRIP)], m_send.at[r, j])
-
-    def settle(r):
-        return pltpu.make_async_copy(summed.at[r], own_ref.at[:, pl.ds(r * STRIP, STRIP)], out_sem.at[r])
-
-    for r in range(AHEAD):
-        begin(r)
-    for r in range(CHUNKS):
-        @pl.loop(1, n_tile)
-        def _(s):
-            source = lax.rem(me + n_tile - lax.rem(s * STRIDE, n_tile), n_tile)
+    def keep(u, j):
+        return pltpu.make_async_copy(summed[u].at[j], mirror_ref.at[j, span(u)], m_send.at[u, j])
+
+    def settle(u):
+        return pltpu.make_async_copy(summed[u], own_ref.at[:, span(u)], out_sem.at[u // 2])
+
+    begin(0)
+    begin(1)
+    for u in range(units):
+        length = BACK[u // 2]
+        table = (u % 2) * 4
+
+        @pl.loop(1, peers)
+        def _(k):
             pltpu.make_async_remote_copy(
-                src_ref=src_ref.at[me, :, pl.ds(r * STRIP, STRIP)], dst_ref=arrived[r].at[pl.ds(source * CAP, CAP)],
-                send_sem=t_send.at[r, s], recv_sem=t_recv.at[r, s],
-                device_id={"tile": source, "aux": aux}, device_id_type=MESH).wait_recv()
-
-        own(r).wait()
+                src_ref=src_ref.at[me, :, span(u)], dst_ref=arrived[u].at[pl.ds(k * CAP, CAP)],
+                send_sem=t_send.at[u, k], recv_sem=t_recv.at[u, k],
+                device_id={"tile": served(me, k, n_tile), "aux": aux}, device_id_type=MESH).wait_recv()
+
+        own(u).wait()
 
         def add(i, carry):
-            for u in range(4):
-                k = i * 4 + u
-                carry = jnp.where(order_ref[1, k] > 0, 0.0, carry) + arrived[r][order_ref[0, k]]
-                running[k] = carry
+            for v in range(4):
+                k = i * 4 + v
+                carry = jnp.where(order_ref[table + 1, k] > 0, 0.0, carry) + arrived[u][order_ref[table, k]]
+                running[k, 0:length] = carry
             return carry
 
-        lax.fori_loop(0, slots // 4, add, jnp.zeros((STRIP, TILE), jnp.float32))
+        lax.fori_loop(0, peers * CAP // 4, add, jnp.zeros((length, TILE), jnp.float32))
 
         @pl.loop(0, n_tile)
         def _(b):
-            rows[r, b] = jnp.where(order_ref[3, b] > 0, running[order_ref[2, b]], 0.0)
-
-        first_up, first_down, second_up, second_down = steps(r)
+            rows[u][b] = jnp.where(order_ref[table + 3, b] > 0, running[order_ref[table + 2, b], 0:length], 0.0)
+
+        first_up, first_down, second_up, second_down = steps(u)
         first_up.start()
         first_down.start()
-        if r + AHEAD < CHUNKS:
-            begin(r + AHEAD)
+        if u + 2 < units:
+            begin(u + 2)
 
         @pl.loop(0, half)
         def _(j):
-            outgoing[r, 0, half + j] = rows[r, up * per + half + j]
-            outgoing[r, 1, j] = rows[r, down * per + j]
+            outgoing[u][0, half + j] = rows[u][up * per + half + j]
+            outgoing[u][1, j] = rows[u][down * per + j]
 
         first_up.wait_recv()
 
         @pl.loop(0, half)
         def _(j):
-            outgoing[r, 0, j] = rows[r, up * per + j] + half_up[r, j]
+            outgoing[u][0, j] = rows[u][up * per + j] + half_up[u][j]
 
         second_up.start()
         first_down.wait_recv()
 
         @pl.loop(0, half)
         def _(j):
-            outgoing[r, 1, half + j] = rows[r, down * per + half + j] + half_down[r, j]
+            outgoing[u][1, half + j] = rows[u][down * per + half + j] + half_down[u][j]
 
         second_down.start()
         second_up.wait_recv()
         second_down.wait_recv()
-
-        @pl.loop(0, per)
-        def _(j):
-            summed[r, j] = rows[r, aux * per + j] + (full_up[r, j] + full_down[r, j])
-            mine = alike & (j == slot)
-
-            @pl.when(jnp.logical_not(mine))
-            def _():
-                send(r, j).start()
-
-            @pl.when(mine)
-            def _():
-                keep(r, j).start()
-
-        settle(r).start()
-
-    for r in range(CHUNKS):
-        @pl.loop(1, n_tile)
-        def _(s):
-            far(r, s).wait_send()
-
-        @pl.loop(0, per)
-        def _(j):
-            mine = alike & (j == slot)
-
-            @pl.when(jnp.logical_not(mine))
-            def _():
-                pltpu.make_async_remote_copy(
-                    src_ref=summed.at[r, j], dst_ref=mirror_ref.at[j, pl.ds(r * STRIP, STRIP)],
-                    send_sem=m_send.at[r, j], recv_sem=m_recv.at[r, j],
-                    device_id={"tile": aux * per + j, "aux": block}, device_id_type=MESH).wait_recv()
-                send(r, j).wait_send()
-
-            @pl.when(mine)
-            def _():
-                keep(r, j).wait()
-
-        settle(r).wait()
-        for copy in steps(r):
+        if u % 2 == 0:
+            @pl.loop(0, per)
+            def _(j):
+                summed[u][j] = rows[u][aux * per + j] + (full_up[u][j] + full_down[u][j])
+
+            swap(u // 2).start()
+        else:
+            swap(u // 2).wait_recv()
+
+            @pl.loop(0, per)
+            def _(j):
+                summed[u][j] = (rows[u][aux * per + j] + swapped[u // 2][j]) + (full_up[u][j] + full_down[u][j])
+                mine = alike & (j == slot)
+
+                @pl.when(jnp.logical_not(mine))
+                def _():
+                    send(u, j).start()
+
+                @pl.when(mine)
+                def _():
+                    keep(u, j).start()
+
+            settle(u).start()
+
+    for u in range(units):
+        @pl.loop(1, peers)
+        def _(k):
+            far(u, k).wait_send()
+
+        for copy in steps(u):
             copy.wait_send()
+        if u % 2 == 0:
+            swap(u // 2).wait_send()
+        else:
+            @pl.loop(0, per)
+            def _(j):
+                mine = alike & (j == slot)
+
+                @pl.when(jnp.logical_not(mine))
+                def _():
+                    pltpu.make_async_remote_copy(
+                        src_ref=summed[u].at[j], dst_ref=mirror_ref.at[j, span(u)],
+                        send_sem=m_send.at[u, j], recv_sem=m_recv.at[u, j],
+                        device_id={"tile": aux * per + j, "aux": block}, device_id_type=MESH).wait_recv()
+                    send(u, j).wait_send()
+
+                @pl.when(mine)
+                def _():
+                    keep(u, j).wait()
+
+            settle(u).wait()
 
 
 def return_partials(order, outbound, n_tile, n_aux):
     per = n_tile // n_aux
-    strips = lambda *lead: pltpu.VMEM(lead + (STRIP, TILE), jnp.float32)
+    peers = n_tile // 2
+    parts = len(BACK)
+    units = 2 * parts
+    lengths = [n for n in BACK for _ in range(2)]
     shape = jax.ShapeDtypeStruct((per, TILE, TILE), jnp.float32)
+    leads = [(peers * CAP,), (n_tile,), (per // 2,), (per // 2,), (per,), (per,), (2, per), (per,)]
     return pl.pallas_call(
         functools.partial(return_kernel, n_tile, n_aux),
         out_shape=(shape, shape),
         in_specs=[pl.BlockSpec(memory_space=pltpu.SMEM), pl.BlockSpec(memory_space=pl.ANY)],
         out_specs=(pl.BlockSpec(memory_space=pl.ANY), pl.BlockSpec(memory_space=pl.ANY)),
-        scratch_shapes=[strips(n_tile * CAP)] * CHUNKS + [
-            strips(n_tile * CAP), strips(CHUNKS, n_tile),
-            strips(CHUNKS, per // 2), strips(CHUNKS, per // 2), strips(CHUNKS, per), strips(CHUNKS, per),
-            strips(CHUNKS, 2, per), strips(CHUNKS, per),
-            pltpu.SemaphoreType.DMA((CHUNKS, n_tile)),
-            pltpu.SemaphoreType.DMA((CHUNKS, n_tile)),
-            pltpu.SemaphoreType.DMA((CHUNKS, 4)),
-            pltpu.SemaphoreType.DMA((CHUNKS, 4)),
-            pltpu.SemaphoreType.DMA((CHUNKS, per)),
-            pltpu.SemaphoreType.DMA((CHUNKS, per)),
-            pltpu.SemaphoreType.DMA((CHUNKS,)),
-            pltpu.SemaphoreType.DMA((CHUNKS,)),
+        scratch_shapes=[pltpu.VMEM(lead + (n, TILE), jnp.float32) for lead in leads for n in lengths]
+        + [pltpu.VMEM((per, n, TILE), jnp.float32) for n in BACK]
+        + [
+            pltpu.VMEM((peers * CAP, max(BACK), TILE), jnp.float32),
+            pltpu.SemaphoreType.DMA((units, peers)),
+            pltpu.SemaphoreType.DMA((units, peers)),
+            pltpu.SemaphoreType.DMA((units, 4)),
+            pltpu.SemaphoreType.DMA((units, 4)),
+            pltpu.SemaphoreType.DMA((units, per)),
+            pltpu.SemaphoreType.DMA((units, per)),
+            pltpu.SemaphoreType.DMA((parts,)),
+            pltpu.SemaphoreType.DMA((parts,)),
+            pltpu.SemaphoreType.DMA((units,)),
+            pltpu.SemaphoreType.DMA((parts,)),
         ],
         compiler_params=pltpu.CompilerParams(collective_id=1, has_side_effects=True, vmem_limit_bytes=VMEM_BYTES),
         name="return_partials",
@@ -541,7 +572,14 @@
     own_source = lax.dynamic_index_in_dim(sources, me, 0, False)
     own_target = lax.dynamic_index_in_dim(targets, me, 0, False)
     send_cols = jnp.concatenate([slot_columns(sources, columns, me), slot_columns(sources, columns, opposite(me))])
-    sum_cols = slot_columns(targets, target_cols, me).reshape(-1)
+    sources_k = served(me, jnp.arange(n_tile // 2, dtype=jnp.int32), n_tile)
+    pick = sources_k[:, None] == jnp.arange(n_tile, dtype=jnp.int32)[None, :]
+
+    def order_for(row):
+        slot_cols = slot_columns(targets, target_cols, row)
+        cols = jnp.sum(jnp.where(pick[:, :, None], slot_cols[None] + 1, 0), axis=1) - 1
+        return column_order(cols.reshape(-1), n_tile)
+
     table = jnp.stack([
         own_source * CAP + ranks_of(own_source),
         slot_pairs[:, 0],
@@ -552,7 +590,7 @@
     incoming = fetch_density(density, jnp.maximum(send_cols, 0), n_tile, n_aux)
     outbound = run_tasks(table, incoming.reshape(slots, TILE, TILE), factors, slots)
     own, mirror = return_partials(
-        column_order(sum_cols, n_tile), outbound.reshape(n_tile, CAP, TILE, TILE), n_tile, n_aux)
+        jnp.concatenate([order_for(opposite(me)), order_for(me)]), outbound.reshape(n_tile, CAP, TILE, TILE), n_tile, n_aux)
     return finish(jnp.stack([me, aux]).astype(jnp.int32), own, mirror, orthogonalizers)
 
 

time: 453 us -> 410 us (0.905)
  Pallas kernels: 438 us -> 395 us
    pallas_call x1, Pallas kernels: 246 us -> 204 us  [return_partials(): pl.pallas_call(functools.partial(return_kernel, n_tile, n_aux), out_shape...]
where the time goes in v4:
time: 410 us; the launch traced here: 409 us
  Pallas kernels  395 us (96%)
  other arithmetic  10.1 us (2%)
    pallas_call x1, Pallas kernels, return_partials(): pl.pallas_call(functools.partial(return_kernel, n_tile, n_aux), out_shape...  204 us
    pallas_call x1, Pallas kernels, fetch_density(): pl.pallas_call(functools.partial(density_kernel, n_tile, n_aux), out_shap...  150 us
    pallas_call x1, Pallas kernels, run_tasks(): pl.pallas_call(functools.partial(task_kernel, aux_funcs // 2), out_shape=...  35.8 us

profile of v4, /device:TPU:22, one launch (start us, length us, event | category | flops | bytes accessed | tf_op | source)
XLA Modules:
  0.0 409.1 jit_solution(9454414815183723401)
XLA Ops:
  0.0 0.6 pad_add_fusion.1.place
  0.6 0.8 slice_bitcast_fusion.1
  1.4 0.1 iota_compare_fusion.8
  1.5 0.5 broadcast.452
  2.0 1.5 reduce.14
  3.5 1.5 reduce.15
  5.0 1.5 reduce.12
  6.4 1.5 reduce.13
  7.9 0.1 reshape.387
  8.1 0.2 convert_reduce_fusion.6
  8.3 0.1 copy.37
  8.4 0.1 reshape.389
  8.5 0.2 convert_reduce_fusion.7
  8.8 0.1 copy.41
  8.8 0.6 pad_add_fusion.table
  9.4 0.3 convert_reduce_fusion
  9.8 0.1 reshape.388
  10.0 0.1 copy.45
  10.1 0.1 select_reduce_fusion.1
  10.3 0.1 copy.39
  10.4 0.1 sub.88
  10.5 0.1 copy.40
  10.6 0.1 sub.95
  10.7 0.2 fusion.7
  10.9 0.2 convert_reduce_fusion.2
  11.1 0.1 fusion.6
  11.2 0.1 select_reduce_fusion
  11.4 0.2 fusion.5
  11.6 0.2 convert_reduce_fusion.4
  11.8 0.1 fusion.4
  11.9 0.1 select_reduce_fusion.2
  12.0 0.6 concatenate.14.order_ref
  12.6 0.1 reshape.390
  12.8 0.1 copy.46
  12.9 0.1 add_add_fusion.2
  13.0 0.1 copy.43
  13.1 0.6 broadcast_maximum_fusion.cols_ref
  13.7 150.2 %fetch_density.1 = f32[64,2,128,128]{3,2,1,0:T(8,128)} custom-call(s32[128,2]{1,0:T(8,128)} %broadcast_maximum_fusion.cols_ref, f32[128,2048]{1,0:T(8,128)} %dens_ref.1), custom_call_target="tpu_custom_call" | custom-call | tf_op jit(solution)/shard_map/fetch_density/pallas_call | solution.py:204
  164.0 35.8 %run_tasks.1 = f32[128,128,128]{2,1,0:T(8,128)} custom-call(s32[4,32]{1,0:T(4,128)} %pad_add_fusion.table, f32[128,128,128]{2,1,0:T(8,128)} %bitcast.92, f32[6,2048,128]{2,1,0:T(8,128)} %bitcast.93), custom_call_target="tpu_custom_call" | custom-call | tf_op jit(solution)/shard_map/run_tasks/pallas_call | solution.py:259
  199.7 203.6 %return_partials.1 = (f32[16,128,128]{2,1,0:T(8,128)}, f32[16,128,128]{2,1,0:T(8,128)}) custom-call(s32[8,64]{1,0:T(8,128)} %concatenate.14.order_ref, f32[64,2,128,128]{3,2,1,0:T(8,128)} %bitcast.91), custom_call_target="tpu_custom_call" | custom-call | tf_op jit(solution)/shard_map/return_partials/pallas_call | solution.py:481
  403.3 5.8 %finish.1 = f32[128,2048]{1,0:T(8,128)} custom-call(s32[2]{0:T(128)} %pad_add_fusion.1.place, f32[16,128,128]{2,1,0:T(8,128)} %get-tuple-element.7.own_ref, f32[16,128,128]{2,1,0:T(8,128)} %get-tuple-element.8.mirror_ref, f32[8192,128]{1,0:T(8,128)} %right_ref.1, f32[8192,128]{1,0:T(8,128)} %right_ref.1), custom_call_target="tpu_custom_call" | custom-call | tf_op jit(solution)/shard_map/finish/pallas_call | solution.py:530
  (34 shorter events, 0.4 us)

commit v5 on v4

--- a/solution.py
+++ b/solution.py
@@ -15,7 +15,8 @@
 ORDER = 13
 ROWS = (48, 80)
 SPANS = [(sum(ROWS[:r]), n) for r, n in enumerate(ROWS)]
-BACK = (56, 40, 32)
+BACK = (48, 40, 24, 16)
+AHEAD = 3
 BACK_SPANS = [(sum(BACK[:r]), n) for r, n in enumerate(BACK)]
 
 
@@ -222,32 +223,34 @@
     )(cols, density)
 
 
-def task_kernel(pair_count, table, dens_ref, fact_ref, out_ref, split):
+def task_kernel(pair_count, table, dens_ref, fact_ref, out_ref, split, lhs):
     q = pl.program_id(0)
+    last = pl.num_programs(0) - 2
+    now = lax.rem(q, 2)
 
     @pl.when(q == 0)
     def _():
+        lhs[1] = jnp.zeros(lhs.shape[1:], lhs.dtype)
+
         @pl.loop(0, fact_ref.shape[0])
         def _(slot):
-            @pl.loop(0, pair_count)
-            def _(p):
-                rows = pl.ds(pl.multiple_of(p * 2 * TILE, 2 * TILE), 2 * TILE)
+            for p in range(pair_count):
+                rows = slice(p * 2 * TILE, (p + 1) * 2 * TILE)
                 top, rest = halves(fact_ref[slot, rows, :])
                 split[slot, rows, 0:TILE] = top
                 split[slot, rows, TILE:2 * TILE] = rest
 
-    left, right = table[1, q], table[2, q]
+    left, right = table[1, jnp.minimum(q, last)], table[2, jnp.maximum(q - 1, 0)]
     top, rest = halves(dens_ref[0])
     row = jnp.concatenate([top, rest], axis=1)
     weights = jnp.concatenate([row, row], axis=0)
-    total = jnp.zeros((2 * TILE, 2 * TILE), jnp.float32)
+    total = jnp.dot(lhs[1 - now], split[right], preferred_element_type=jnp.float32)
     for p in range(pair_count):
         rows = slice(p * 2 * TILE, (p + 1) * 2 * TILE)
         wide = jnp.dot(split[left, rows, :], weights, preferred_element_type=jnp.float32)
         top, rest = halves(wide[:, :TILE] + wide[:, TILE:])
-        lhs = jnp.concatenate(
+        lhs[now, :, rows] = jnp.concatenate(
             [jnp.concatenate([top[:TILE], top[TILE:]], axis=1), jnp.concatenate([rest[:TILE], rest[TILE:]], axis=1)], axis=0)
-        total = total + jnp.dot(lhs, split[right, rows, :], preferred_element_type=jnp.float32)
     tall = total[:, :TILE] + total[:, TILE:]
     out_ref[0] = tall[:TILE] + tall[TILE:]
 
@@ -261,13 +264,16 @@
         out_shape=jax.ShapeDtypeStruct((slots, TILE, TILE), jnp.float32),
         grid_spec=pltpu.PrefetchScalarGridSpec(
             num_scalar_prefetch=1,
-            grid=(task_count,),
+            grid=(task_count + 1,),
             in_specs=[
-                pl.BlockSpec((1, TILE, TILE), lambda q, t: (t[0, q], 0, 0)),
+                pl.BlockSpec((1, TILE, TILE), lambda q, t: (t[0, jnp.minimum(q, task_count - 1)], 0, 0)),
                 pl.BlockSpec(flat.shape, lambda q, t: (0, 0, 0), pipeline_mode=pl.Buffered(1)),
             ],
-            out_specs=pl.BlockSpec((1, TILE, TILE), lambda q, t: (t[3, q], 0, 0)),
-            scratch_shapes=[pltpu.VMEM((slot_count, aux_funcs * TILE, 2 * TILE), jnp.bfloat16)],
+            out_specs=pl.BlockSpec((1, TILE, TILE), lambda q, t: (t[3, jnp.maximum(q - 1, 0)], 0, 0)),
+            scratch_shapes=[
+                pltpu.VMEM((slot_count, aux_funcs * TILE, 2 * TILE), jnp.bfloat16),
+                pltpu.VMEM((2, 2 * TILE, aux_funcs * TILE), jnp.bfloat16),
+            ],
         ),
         compiler_params=pltpu.CompilerParams(vmem_limit_bytes=VMEM_BYTES),
         name="run_tasks",
@@ -362,9 +368,7 @@
     def settle(u):
         return pltpu.make_async_copy(summed[u], own_ref.at[:, span(u)], out_sem.at[u // 2])
 
-    begin(0)
-    begin(1)
-    for u in range(units):
+    def collect(u):
         length = BACK[u // 2]
         table = (u % 2) * 4
 
@@ -376,6 +380,8 @@
                 device_id={"tile": served(me, k, n_tile), "aux": aux}, device_id_type=MESH).wait_recv()
 
         own(u).wait()
+        if u + AHEAD < units:
+            begin(u + AHEAD)
 
         def add(i, carry):
             for v in range(4):
@@ -390,17 +396,17 @@
         def _(b):
             rows[u][b] = jnp.where(order_ref[table + 3, b] > 0, running[order_ref[table + 2, b], 0:length], 0.0)
 
-        first_up, first_down, second_up, second_down = steps(u)
+        first_up, first_down, _, _ = steps(u)
         first_up.start()
         first_down.start()
-        if u + 2 < units:
-            begin(u + 2)
 
         @pl.loop(0, half)
         def _(j):
             outgoing[u][0, half + j] = rows[u][up * per + half + j]
             outgoing[u][1, j] = rows[u][down * per + j]
 
+    def pass_on(u):
+        first_up, first_down, second_up, second_down = steps(u)
         first_up.wait_recv()
 
         @pl.loop(0, half)
@@ -415,6 +421,9 @@
             outgoing[u][1, half + j] = rows[u][down * per + half + j] + half_down[u][j]
 
         second_down.start()
+
+    def conclude(u):
+        _, _, second_up, second_down = steps(u)
         second_up.wait_recv()
         second_down.wait_recv()
         if u % 2 == 0:
@@ -440,6 +449,15 @@
                     keep(u, j).start()
 
             settle(u).start()
+
+    for u in range(AHEAD):
+        begin(u)
+    for u in range(units):
+        collect(u)
+        if u > 0:
+            conclude(u - 1)
+        pass_on(u)
+    conclude(units - 1)
 
     for u in range(units):
         @pl.loop(1, peers)
@@ -563,12 +581,14 @@
     me, aux = lax.axis_index("tile"), lax.axis_index("aux")
     tasks = slot_pairs.shape[0]
 
-    def group(rows):
-        grid = rows.reshape(n_tile, n_aux, tasks)
-        return lax.dynamic_index_in_dim(grid, aux, 1, False)
-
-    sources, columns = group(density_source), group(density_column)
-    targets, target_cols = group(target_row), group(target_column)
+    packed = density_source
+    for other in (density_column, target_row, target_column):
+        packed = packed * n_tile + other
+    packed = lax.dynamic_index_in_dim(packed.reshape(n_tile, n_aux, tasks), aux, 1, False)
+    target_cols = packed % n_tile
+    targets = (packed // n_tile) % n_tile
+    columns = (packed // n_tile ** 2) % n_tile
+    sources = packed // n_tile ** 3
     own_source = lax.dynamic_index_in_dim(sources, me, 0, False)
     own_target = lax.dynamic_index_in_dim(targets, me, 0, False)
     send_cols = jnp.concatenate([slot_columns(sources, columns, me), slot_columns(sources, columns, opposite(me))])

time: 410 us -> 401 us (0.978); the launches traced: 409 us -> 394 us
  Pallas kernels: 395 us -> 385 us
  other arithmetic: 10.1 us -> 5.97 us
    pallas_call x1, Pallas kernels: 204 us -> 197 us  [return_partials(): pl.pallas_call(functools.partial(return_kernel, n_tile, n_aux), out_shape...]
    unnamed x4 -> x0, other arithmetic: 5.93 us -> none
where the time goes in v5:
time: 401 us; the launch traced here: 394 us
  Pallas kernels  385 us (96%)
  other arithmetic  5.97 us (1%)
    pallas_call x1, Pallas kernels, return_partials(): pl.pallas_call(functools.partial(return_kernel, n_tile, n_aux), out_shape...  197 us
    pallas_call x1, Pallas kernels, fetch_density(): pl.pallas_call(functools.partial(density_kernel, n_tile, n_aux), out_shap...  150 us
    pallas_call x1, Pallas kernels, run_tasks(): pl.pallas_call(functools.partial(task_kernel, aux_funcs // 2), out_shape=...  32.1 us

profile of v5, /device:TPU:22, one launch (start us, length us, event | category | flops | bytes accessed | tf_op | source)
XLA Modules:
  0.0 393.6 jit_solution(15534944286336952038)
XLA Ops:
  0.0 0.6 pad_add_fusion.1.place
  0.6 0.8 slice_bitcast_fusion.1
  1.4 0.1 iota_compare_fusion.8
  1.5 0.9 add_reduce_fusion
  2.4 0.1 reshape.386
  2.5 0.3 and_select_fusion.1
  2.8 0.1 copy.37
  2.9 0.2 and_select_fusion
  3.0 0.1 copy.43
  3.1 0.1 fusion.5
  3.2 0.1 broadcast_compare_fusion.2
  3.3 0.2 convert_reduce_fusion.7
  3.5 0.2 convert_reduce_fusion.6
  3.7 0.6 pad_add_fusion.table
  4.3 0.1 copy.42
  4.3 0.1 copy.36
  4.4 0.4 convert_reduce_fusion
  4.8 0.1 copy.44
  4.9 0.2 select_reduce_fusion.3
  5.0 0.1 add_add_fusion.2
  5.1 0.1 copy.38
  5.2 0.2 select_reduce_fusion.7
  5.5 0.1 select_reduce_fusion.5
  5.6 0.1 copy.40
  5.7 0.1 sub.108
  5.8 0.1 copy.41
  5.9 0.1 sub.115
  6.0 0.2 fusion.14
  6.2 0.2 convert_reduce_fusion.2
  6.4 0.1 fusion.13
  6.5 0.1 select_reduce_fusion.4
  6.7 0.2 fusion.12
  6.9 0.2 convert_reduce_fusion.4
  7.1 0.1 fusion.11
  7.2 0.1 select_reduce_fusion.8
  7.3 0.6 concatenate.14.order_ref
  7.9 0.1 copy.46
  8.0 0.6 broadcast_maximum_fusion.cols_ref
  8.7 150.2 %fetch_density.1 = f32[64,2,128,128]{3,2,1,0:T(8,128)} custom-call(s32[128,2]{1,0:T(8,128)} %broadcast_maximum_fusion.cols_ref, f32[128,2048]{1,0:T(8,128)} %dens_ref.1), custom_call_target="tpu_custom_call" | custom-call | tf_op jit(solution)/shard_map/fetch_density/pallas_call | solution.py:205
  158.9 32.1 %run_tasks.1 = f32[128,128,128]{2,1,0:T(8,128)} custom-call(s32[4,32]{1,0:T(4,128)} %pad_add_fusion.table, f32[128,128,128]{2,1,0:T(8,128)} %bitcast.55, f32[6,2048,128]{2,1,0:T(8,128)} %bitcast.56), custom_call_target="tpu_custom_call" | custom-call | tf_op jit(solution)/shard_map/run_tasks/pallas_call | solution.py:262
  191.0 196.8 %return_partials.1 = (f32[16,128,128]{2,1,0:T(8,128)}, f32[16,128,128]{2,1,0:T(8,128)}) custom-call(s32[8,64]{1,0:T(8,128)} %concatenate.14.order_ref, f32[64,2,128,128]{3,2,1,0:T(8,128)} %bitcast.54), custom_call_target="tpu_custom_call" | custom-call | tf_op jit(solution)/shard_map/return_partials/pallas_call | solution.py:499
  387.8 5.8 %finish.1 = f32[128,2048]{1,0:T(8,128)} custom-call(s32[2]{0:T(128)} %pad_add_fusion.1.place, f32[16,128,128]{2,1,0:T(8,128)} %get-tuple-element.7.own_ref, f32[16,128,128]{2,1,0:T(8,128)} %get-tuple-element.8.mirror_ref, f32[8192,128]{1,0:T(8,128)} %right_ref.1, f32[8192,128]{1,0:T(8,128)} %right_ref.1), custom_call_target="tpu_custom_call" | custom-call | tf_op jit(solution)/shard_map/finish/pallas_call | solution.py:548
  (26 shorter events, 0.2 us)

commit v6 on v5

--- a/solution.py
+++ b/solution.py
@@ -13,10 +13,10 @@
 RING = 8
 CORES = 2
 ORDER = 13
-ROWS = (48, 80)
+ROWS = (32, 48, 48)
 SPANS = [(sum(ROWS[:r]), n) for r, n in enumerate(ROWS)]
 BACK = (48, 40, 24, 16)
-AHEAD = 3
+AHEAD = 2
 BACK_SPANS = [(sum(BACK[:r]), n) for r, n in enumerate(BACK)]
 
 
@@ -50,30 +50,38 @@
     return (x * RING + z) * CORES + core
 
 
-def opposite(tile):
+def copy_at(tile):
     x, z, core = spot_of(tile)
-    return tile_of(x, lax.rem(z + RING // 2, RING), core)
-
-
-def reach(turn, core):
-    far = jnp.where(core == 0, 2, RING - 2)
+    return tile_of(x, lax.rem(z + 3 + (RING - 6) * core, RING), core)
+
+
+def copy_of(tile):
+    x, z, core = spot_of(tile)
+    return tile_of(x, lax.rem(z + RING - 3 - (RING - 6) * core, RING), core)
+
+
+def reach(turn, core, copy):
+    far = jnp.where(core == 0, RING - 2, 2)
+    if copy:
+        far = RING - far
     return jnp.where(turn == 3, far, jnp.where(turn == 2, RING - 1, turn))
 
 
-def served(tile, k, n_tile):
+def served(tile, k, n_tile, copy):
     x, z, core = spot_of(tile)
     across = n_tile // (RING * CORES)
     to_core = lax.rem(core + lax.rem(k, CORES), CORES)
     turn = lax.rem(k // CORES, 4)
-    return tile_of(lax.rem(x + k // (4 * CORES), across), lax.rem(z + reach(turn, core), RING), to_core)
-
-
-def holder(tile, k, n_tile):
+    return tile_of(lax.rem(x + k // (4 * CORES), across), lax.rem(z + reach(turn, core, copy), RING), to_core)
+
+
+def holder(tile, k, n_tile, copy):
     x, z, core = spot_of(tile)
     across = n_tile // (RING * CORES)
     from_core = lax.rem(core + CORES - lax.rem(k, CORES), CORES)
     turn = lax.rem(k // CORES, 4)
-    return tile_of(lax.rem(x + across - k // (4 * CORES), across), lax.rem(z + RING - reach(turn, from_core), RING), from_core)
+    z_from = lax.rem(z + RING - reach(turn, from_core, copy), RING)
+    return tile_of(lax.rem(x + across - k // (4 * CORES), across), z_from, from_core)
 
 
 def density_kernel(n_tile, n_aux, cols_ref, dens_ref, out_ref, *scratch):
@@ -82,8 +90,7 @@
     y_send, y_recv, z_send, z_recv, t_send, t_recv, own_sem = scratch[4 * parts:]
     me = lax.axis_index("tile")
     aux = lax.axis_index("aux")
-    far_side = opposite(me)
-    homes = [me] * parts + [far_side] * parts
+    homes = [me] * parts + [copy_of(me)] * parts
     spans = SPANS * 2
     up, down = lax.rem(aux + 1, n_aux), lax.rem(aux + n_aux - 1, n_aux)
     across = lax.rem(aux + 2, n_aux)
@@ -113,7 +120,7 @@
         mine = pl.ds(aux * per, per)
         return pltpu.make_async_remote_copy(
             src_ref=slabs[r].at[mine], dst_ref=slabs[parts + r].at[mine], send_sem=z_send.at[r], recv_sem=z_recv.at[r],
-            device_id={"tile": far_side, "aux": aux}, device_id_type=MESH)
+            device_id={"tile": copy_at(me), "aux": aux}, device_id_type=MESH)
 
     def home_rows(tile, r):
         return out_ref.at[tile, :, pl.ds(*spans[r])]
@@ -122,7 +129,7 @@
         return pltpu.make_async_remote_copy(
             src_ref=outgoing[r].at[k], dst_ref=home_rows(homes[r], r),
             send_sem=t_send.at[r, k], recv_sem=t_recv.at[r, k],
-            device_id={"tile": served(me, k, n_tile), "aux": aux}, device_id_type=MESH)
+            device_id={"tile": served(me, k, n_tile, r >= parts), "aux": aux}, device_id_type=MESH)
 
     def own(r):
         return pltpu.make_async_copy(outgoing[r].at[0], home_rows(homes[r], r), own_sem.at[r])
@@ -147,7 +154,7 @@
         @pl.loop(0, peers)
         def _(s):
             k = lax.rem(s * ORDER, peers)
-            dest = base + served(me, k, n_tile)
+            dest = base + served(me, k, n_tile, r >= parts)
             for level in range(CAP):
                 outgoing[r][k, level] = slabs[r][cols_ref[dest, level]]
 
@@ -161,30 +168,23 @@
         swap(r).wait_recv()
         first(parts + r)
 
-    first(0)
-    swap(0).start()
-    first(1)
-    swap(1).start()
+    for r in range(parts):
+        first(r)
+        swap(r).start()
     second(0)
-    gathered(0)
-    send_all(0)
-    second(1)
-    step_copy(0)
-    gathered(1)
-    second(2)
-    send_all(1)
-    gathered(2)
-    step_copy(1)
-    send_all(2)
-    second(3)
-    gathered(3)
-    send_all(3)
+    for r in range(2 * parts):
+        gathered(r)
+        if r + 1 < 2 * parts:
+            second(r + 1)
+        send_all(r)
+        if r < parts:
+            step_copy(r)
 
     for r in range(2 * parts):
         @pl.loop(1, peers)
         def _(k):
-            source = holder(me, k, n_tile)
-            home = source if r < parts else opposite(source)
+            source = holder(me, k, n_tile, r >= parts)
+            home = source if r < parts else copy_of(source)
             pltpu.make_async_remote_copy(
                 src_ref=outgoing[r].at[k], dst_ref=home_rows(home, r),
                 send_sem=t_send.at[r, k], recv_sem=t_recv.at[r, k],
@@ -289,7 +289,6 @@
     (running, t_send, t_recv, y_send, y_recv, m_send, m_recv, z_send, z_recv, own_sem, out_sem) = scratch[8 * units + parts:]
     me = lax.axis_index("tile")
     aux = lax.axis_index("aux")
-    far_side = opposite(me)
     up, down = lax.rem(aux + 1, n_aux), lax.rem(aux + n_aux - 1, n_aux)
     across = lax.rem(aux + 2, n_aux)
     per = n_tile // n_aux
@@ -319,10 +318,10 @@
         return pl.ds(*BACK_SPANS[u // 2])
 
     def home_of(tile, u):
-        return opposite(tile) if u % 2 == 0 else tile
+        return copy_of(tile) if u % 2 == 0 else tile
 
     def far(u, k):
-        dest = holder(me, k, n_tile)
+        dest = holder(me, k, n_tile, u % 2 == 0)
         return pltpu.make_async_remote_copy(
             src_ref=src_ref.at[home_of(dest, u), :, span(u)], dst_ref=arrived[u].at[pl.ds(k * CAP, CAP)],
             send_sem=t_send.at[u, k], recv_sem=t_recv.at[u, k],
@@ -354,7 +353,7 @@
     def swap(p):
         return pltpu.make_async_remote_copy(
             src_ref=summed[2 * p], dst_ref=swapped[p], send_sem=z_send.at[p], recv_sem=z_recv.at[p],
-            device_id={"tile": far_side, "aux": aux}, device_id_type=MESH)
+            device_id={"tile": copy_of(me), "aux": aux}, device_id_type=MESH)
 
     def send(u, j):
         return pltpu.make_async_remote_copy(
@@ -377,7 +376,7 @@
             pltpu.make_async_remote_copy(
                 src_ref=src_ref.at[me, :, span(u)], dst_ref=arrived[u].at[pl.ds(k * CAP, CAP)],
                 send_sem=t_send.at[u, k], recv_sem=t_recv.at[u, k],
-                device_id={"tile": served(me, k, n_tile), "aux": aux}, device_id_type=MESH).wait_recv()
+                device_id={"tile": served(me, k, n_tile, u % 2 == 0), "aux": aux}, device_id_type=MESH).wait_recv()
 
         own(u).wait()
         if u + AHEAD < units:
@@ -591,12 +590,12 @@
     sources = packed // n_tile ** 3
     own_source = lax.dynamic_index_in_dim(sources, me, 0, False)
     own_target = lax.dynamic_index_in_dim(targets, me, 0, False)
-    send_cols = jnp.concatenate([slot_columns(sources, columns, me), slot_columns(sources, columns, opposite(me))])
-    sources_k = served(me, jnp.arange(n_tile // 2, dtype=jnp.int32), n_tile)
-    pick = sources_k[:, None] == jnp.arange(n_tile, dtype=jnp.int32)[None, :]
-
-    def order_for(row):
+    send_cols = jnp.concatenate([slot_columns(sources, columns, me), slot_columns(sources, columns, copy_of(me))])
+    places = jnp.arange(n_tile, dtype=jnp.int32)
+
+    def order_for(row, copy):
         slot_cols = slot_columns(targets, target_cols, row)
+        pick = served(me, places[:n_tile // 2], n_tile, copy)[:, None] == places[None, :]
         cols = jnp.sum(jnp.where(pick[:, :, None], slot_cols[None] + 1, 0), axis=1) - 1
         return column_order(cols.reshape(-1), n_tile)
 
@@ -610,7 +609,7 @@
     incoming = fetch_density(density, jnp.maximum(send_cols, 0), n_tile, n_aux)
     outbound = run_tasks(table, incoming.reshape(slots, TILE, TILE), factors, slots)
     own, mirror = return_partials(
-        jnp.concatenate([order_for(opposite(me)), order_for(me)]), outbound.reshape(n_tile, CAP, TILE, TILE), n_tile, n_aux)
+        jnp.concatenate([order_for(copy_of(me), True), order_for(me, False)]), outbound.reshape(n_tile, CAP, TILE, TILE), n_tile, n_aux)
     return finish(jnp.stack([me, aux]).astype(jnp.int32), own, mirror, orthogonalizers)
 
 

time: 401 us -> 382 us (0.953)
  Pallas kernels: 385 us -> 366 us
    pallas_call x1, Pallas kernels: 197 us -> 187 us  [return_partials(): pl.pallas_call(functools.partial(return_kernel, n_tile, n_aux), out_shape...]
    pallas_call x1, Pallas kernels: 150 us -> 141 us  [fetch_density(): pl.pallas_call(functools.partial(density_kernel, n_tile, n_aux), out_shap...]
where the time goes in v6:
time: 382 us; the launch traced here: 375 us
  Pallas kernels  366 us (96%)
  other arithmetic  6.15 us (2%)
    pallas_call x1, Pallas kernels, return_partials(): pl.pallas_call(functools.partial(return_kernel, n_tile, n_aux), out_shape...  187 us
    pallas_call x1, Pallas kernels, fetch_density(): pl.pallas_call(functools.partial(density_kernel, n_tile, n_aux), out_shap...  141 us
    pallas_call x1, Pallas kernels, run_tasks(): pl.pallas_call(functools.partial(task_kernel, aux_funcs // 2), out_shape=...  32.1 us

profile of v6, /device:TPU:22, one launch (start us, length us, event | category | flops | bytes accessed | tf_op | source)
XLA Modules:
  0.0 374.8 jit_solution(10300253100481551271)
XLA Ops:
  0.0 0.6 pad_add_fusion.1.place
  0.7 0.8 slice_bitcast_fusion.1
  1.4 0.1 iota_compare_fusion.7
  1.5 0.1 iota_compare_fusion.9
  1.6 0.9 add_reduce_fusion
  2.5 0.1 reshape.352
  2.7 0.3 and_select_fusion.1
  2.9 0.1 copy.37
  3.0 0.2 and_select_fusion
  3.2 0.1 copy.43
  3.2 0.1 fusion.5
  3.3 0.1 broadcast_compare_fusion.2
  3.4 0.2 convert_reduce_fusion.7
  3.6 0.2 convert_reduce_fusion.6
  3.8 0.6 pad_add_fusion.table
  4.4 0.1 copy.42
  4.4 0.1 copy.36
  4.5 0.4 convert_reduce_fusion
  4.9 0.1 copy.44
  5.0 0.2 select_reduce_fusion.3
  5.2 0.1 add_add_fusion.2
  5.2 0.1 copy.38
  5.3 0.2 select_reduce_fusion.7
  5.5 0.1 select_reduce_fusion.5
  5.7 0.1 select_reduce_fusion.9
  5.8 0.1 copy.40
  5.9 0.1 sub.132
  6.0 0.1 copy.41
  6.1 0.1 sub.139
  6.2 0.2 fusion.14
  6.4 0.2 convert_reduce_fusion.2
  6.6 0.1 fusion.13
  6.7 0.1 select_reduce_fusion.4
  6.9 0.2 fusion.12
  7.1 0.2 convert_reduce_fusion.4
  7.3 0.1 fusion.11
  7.4 0.1 select_reduce_fusion.8
  7.5 0.6 concatenate.14.order_ref
  8.1 0.1 copy.46
  8.2 0.6 broadcast_maximum_fusion.cols_ref
  8.9 140.8 %fetch_density.1 = f32[64,2,128,128]{3,2,1,0:T(8,128)} custom-call(s32[128,2]{1,0:T(8,128)} %broadcast_maximum_fusion.cols_ref, f32[128,2048]{1,0:T(8,128)} %dens_ref.1), custom_call_target="tpu_custom_call" | custom-call | tf_op jit(solution)/shard_map/fetch_density/pallas_call | solution.py:205
  149.6 32.1 %run_tasks.1 = f32[128,128,128]{2,1,0:T(8,128)} custom-call(s32[4,32]{1,0:T(4,128)} %pad_add_fusion.table, f32[128,128,128]{2,1,0:T(8,128)} %bitcast.55, f32[6,2048,128]{2,1,0:T(8,128)} %bitcast.56), custom_call_target="tpu_custom_call" | custom-call | tf_op jit(solution)/shard_map/run_tasks/pallas_call | solution.py:262
  181.8 187.2 %return_partials.1 = (f32[16,128,128]{2,1,0:T(8,128)}, f32[16,128,128]{2,1,0:T(8,128)}) custom-call(s32[8,64]{1,0:T(8,128)} %concatenate.14.order_ref, f32[64,2,128,128]{3,2,1,0:T(8,128)} %bitcast.54), custom_call_target="tpu_custom_call" | custom-call | tf_op jit(solution)/shard_map/return_partials/pallas_call | solution.py:498
  368.9 5.8 %finish.1 = f32[128,2048]{1,0:T(8,128)} custom-call(s32[2]{0:T(128)} %pad_add_fusion.1.place, f32[16,128,128]{2,1,0:T(8,128)} %get-tuple-element.7.own_ref, f32[16,128,128]{2,1,0:T(8,128)} %get-tuple-element.8.mirror_ref, f32[8192,128]{1,0:T(8,128)} %right_ref.1, f32[8192,128]{1,0:T(8,128)} %right_ref.1), custom_call_target="tpu_custom_call" | custom-call | tf_op jit(solution)/shard_map/finish/pallas_call | solution.py:547
  (28 shorter events, 0.2 us)

commit v7 on v6

--- a/solution.py
+++ b/solution.py
@@ -435,7 +435,8 @@
             swap(u // 2).wait_recv()
 
             @pl.loop(0, per)
-            def _(j):
+            def _(turn):
+                j = lax.rem(slot + turn, per)
                 summed[u][j] = (rows[u][aux * per + j] + swapped[u // 2][j]) + (full_up[u][j] + full_down[u][j])
                 mine = alike & (j == slot)
 

time: 382 us -> 381 us (level)
  no operation moved by 1% of the time
where the time goes in v7:
time: 381 us; the launch traced here: 376 us
  Pallas kernels  367 us (96%)
  other arithmetic  6.15 us (2%)
    pallas_call x1, Pallas kernels, return_partials(): pl.pallas_call(functools.partial(return_kernel, n_tile, n_aux), out_shape...  188 us
    pallas_call x1, Pallas kernels, fetch_density(): pl.pallas_call(functools.partial(density_kernel, n_tile, n_aux), out_shap...  141 us
    pallas_call x1, Pallas kernels, run_tasks(): pl.pallas_call(functools.partial(task_kernel, aux_funcs // 2), out_shape=...  32.1 us

profile of v7, /device:TPU:22, one launch (start us, length us, event | category | flops | bytes accessed | tf_op | source)
XLA Modules:
  0.0 376.0 jit_solution(7712048922701338968)
XLA Ops:
  0.0 0.6 pad_add_fusion.1.place
  0.7 0.8 slice_bitcast_fusion.1
  1.4 0.1 iota_compare_fusion.7
  1.5 0.1 iota_compare_fusion.9
  1.6 0.9 add_reduce_fusion
  2.5 0.1 reshape.352
  2.7 0.3 and_select_fusion.1
  2.9 0.1 copy.37
  3.0 0.2 and_select_fusion
  3.2 0.1 copy.43
  3.2 0.1 fusion.5
  3.3 0.1 broadcast_compare_fusion.2
  3.4 0.2 convert_reduce_fusion.7
  3.6 0.2 convert_reduce_fusion.6
  3.8 0.6 pad_add_fusion.table
  4.4 0.1 copy.42
  4.4 0.1 copy.36
  4.5 0.4 convert_reduce_fusion
  4.9 0.1 copy.44
  5.0 0.2 select_reduce_fusion.3
  5.2 0.1 add_add_fusion.2
  5.2 0.1 copy.38
  5.3 0.2 select_reduce_fusion.7
  5.5 0.1 select_reduce_fusion.5
  5.7 0.1 select_reduce_fusion.9
  5.8 0.1 copy.40
  5.9 0.1 sub.132
  6.0 0.1 copy.41
  6.1 0.1 sub.139
  6.2 0.2 fusion.14
  6.4 0.2 convert_reduce_fusion.2
  6.6 0.1 fusion.13
  6.7 0.1 select_reduce_fusion.4
  6.9 0.2 fusion.12
  7.1 0.2 convert_reduce_fusion.4
  7.3 0.1 fusion.11
  7.4 0.1 select_reduce_fusion.8
  7.5 0.6 concatenate.14.order_ref
  8.1 0.1 copy.46
  8.2 0.6 broadcast_maximum_fusion.cols_ref
  8.9 140.8 %fetch_density.1 = f32[64,2,128,128]{3,2,1,0:T(8,128)} custom-call(s32[128,2]{1,0:T(8,128)} %broadcast_maximum_fusion.cols_ref, f32[128,2048]{1,0:T(8,128)} %dens_ref.1), custom_call_target="tpu_custom_call" | custom-call | tf_op jit(solution)/shard_map/fetch_density/pallas_call | solution.py:205
  149.6 32.1 %run_tasks.1 = f32[128,128,128]{2,1,0:T(8,128)} custom-call(s32[4,32]{1,0:T(4,128)} %pad_add_fusion.table, f32[128,128,128]{2,1,0:T(8,128)} %bitcast.55, f32[6,2048,128]{2,1,0:T(8,128)} %bitcast.56), custom_call_target="tpu_custom_call" | custom-call | tf_op jit(solution)/shard_map/run_tasks/pallas_call | solution.py:262
  181.8 188.5 %return_partials.1 = (f32[16,128,128]{2,1,0:T(8,128)}, f32[16,128,128]{2,1,0:T(8,128)}) custom-call(s32[8,64]{1,0:T(8,128)} %concatenate.14.order_ref, f32[64,2,128,128]{3,2,1,0:T(8,128)} %bitcast.54), custom_call_target="tpu_custom_call" | custom-call | tf_op jit(solution)/shard_map/return_partials/pallas_call | solution.py:499
  370.2 5.8 %finish.1 = f32[128,2048]{1,0:T(8,128)} custom-call(s32[2]{0:T(128)} %pad_add_fusion.1.place, f32[16,128,128]{2,1,0:T(8,128)} %get-tuple-element.7.own_ref, f32[16,128,128]{2,1,0:T(8,128)} %get-tuple-element.8.mirror_ref, f32[8192,128]{1,0:T(8,128)} %right_ref.1, f32[8192,128]{1,0:T(8,128)} %right_ref.1), custom_call_target="tpu_custom_call" | custom-call | tf_op jit(solution)/shard_map/finish/pallas_call | solution.py:548
  (28 shorter events, 0.2 us)

commit v8 on v7

--- a/solution.py
+++ b/solution.py
@@ -13,9 +13,10 @@
 RING = 8
 CORES = 2
 ORDER = 13
-ROWS = (32, 48, 48)
+KINDS = 3
+ROWS = (56, 72)
 SPANS = [(sum(ROWS[:r]), n) for r, n in enumerate(ROWS)]
-BACK = (48, 40, 24, 16)
+BACK = (56, 40, 24, 8)
 AHEAD = 2
 BACK_SPANS = [(sum(BACK[:r]), n) for r, n in enumerate(BACK)]
 
@@ -84,19 +85,54 @@
     return tile_of(lax.rem(x + across - k // (4 * CORES), across), z_from, from_core)
 
 
+def turned(z, steps, core):
+    return lax.rem(z + steps * (1 - 2 * core) + RING, RING)
+
+
+def held_at(tile, kind):
+    x, z, core = spot_of(tile)
+    return tile_of(x, turned(z, (0, 3, -2)[kind], core), core)
+
+
+def held_by(tile, kind):
+    x, z, core = spot_of(tile)
+    return tile_of(x, turned(z, (0, -3, 2)[kind], core), core)
+
+
+def fan(n_tile, kind):
+    return n_tile // RING * (2 if kind == 0 else 3)
+
+
+def fed(tile, k, n_tile, kind):
+    x, z, core = spot_of(tile)
+    across, turns = n_tile // (RING * CORES), 2 if kind == 0 else 3
+    turn = lax.rem(k // CORES, turns)
+    to_core = lax.rem(core + lax.rem(k, CORES), CORES)
+    return tile_of(lax.rem(x + k // (turns * CORES), across), turned(z, turn - 3 * (turn // 2), core), to_core)
+
+
+def feeder(tile, k, n_tile, kind):
+    x, z, core = spot_of(tile)
+    across, turns = n_tile // (RING * CORES), 2 if kind == 0 else 3
+    turn = lax.rem(k // CORES, turns)
+    from_core = lax.rem(core + CORES - lax.rem(k, CORES), CORES)
+    z_from = turned(z, 3 * (turn // 2) - turn, from_core)
+    return tile_of(lax.rem(x + across - k // (turns * CORES), across), z_from, from_core)
+
+
 def density_kernel(n_tile, n_aux, cols_ref, dens_ref, out_ref, *scratch):
     parts = len(ROWS)
-    slabs, outgoing = scratch[:2 * parts], scratch[2 * parts:4 * parts]
-    y_send, y_recv, z_send, z_recv, t_send, t_recv, own_sem = scratch[4 * parts:]
+    units = KINDS * parts
+    slabs, outgoing = scratch[:units], scratch[units:2 * units]
+    y_send, y_recv, z_send, z_recv, t_send, t_recv, own_sem = scratch[2 * units:]
     me = lax.axis_index("tile")
     aux = lax.axis_index("aux")
-    homes = [me] * parts + [copy_of(me)] * parts
-    spans = SPANS * 2
+    homes = [held_by(me, u // parts) for u in range(units)]
+    spans = SPANS * KINDS
     up, down = lax.rem(aux + 1, n_aux), lax.rem(aux + n_aux - 1, n_aux)
     across = lax.rem(aux + 2, n_aux)
     per = dens_ref.shape[1] // TILE
     half = per // 2
-    peers = n_tile // 2
     barrier = pltpu.get_barrier_semaphore()
 
     @pl.loop(1, n_tile)
@@ -116,11 +152,12 @@
             src_ref=where, dst_ref=where, send_sem=y_send.at[r, index], recv_sem=y_recv.at[r, index],
             device_id={"tile": me, "aux": other}, device_id_type=MESH)
 
-    def swap(r):
+    def swap(u):
         mine = pl.ds(aux * per, per)
         return pltpu.make_async_remote_copy(
-            src_ref=slabs[r].at[mine], dst_ref=slabs[parts + r].at[mine], send_sem=z_send.at[r], recv_sem=z_recv.at[r],
-            device_id={"tile": copy_at(me), "aux": aux}, device_id_type=MESH)
+            src_ref=slabs[u % parts].at[mine], dst_ref=slabs[u].at[mine],
+            send_sem=z_send.at[u], recv_sem=z_recv.at[u],
+            device_id={"tile": held_at(me, u // parts), "aux": aux}, device_id_type=MESH)
 
     def home_rows(tile, r):
         return out_ref.at[tile, :, pl.ds(*spans[r])]
@@ -129,7 +166,7 @@
         return pltpu.make_async_remote_copy(
             src_ref=outgoing[r].at[k], dst_ref=home_rows(homes[r], r),
             send_sem=t_send.at[r, k], recv_sem=t_recv.at[r, k],
-            device_id={"tile": served(me, k, n_tile, r >= parts), "aux": aux}, device_id_type=MESH)
+            device_id={"tile": fed(me, k, n_tile, r // parts), "aux": aux}, device_id_type=MESH)
 
     def own(r):
         return pltpu.make_async_copy(outgoing[r].at[0], home_rows(homes[r], r), own_sem.at[r])
@@ -149,12 +186,13 @@
         near(r, across, half, half, 3, down).wait_recv()
 
     def send_all(r):
-        base = 0 if r < parts else n_tile
+        base = r // parts * n_tile
+        peers = fan(n_tile, r // parts)
 
         @pl.loop(0, peers)
         def _(s):
             k = lax.rem(s * ORDER, peers)
-            dest = base + served(me, k, n_tile, r >= parts)
+            dest = base + fed(me, k, n_tile, r // parts)
             for level in range(CAP):
                 outgoing[r][k, level] = slabs[r][cols_ref[dest, level]]
 
@@ -164,27 +202,26 @@
 
         own(r).start()
 
-    def step_copy(r):
-        swap(r).wait_recv()
-        first(parts + r)
-
-    for r in range(parts):
+    first(0)
+    for u in range(parts, units):
+        swap(u).start()
+    for r in range(1, parts):
         first(r)
-        swap(r).start()
     second(0)
-    for r in range(2 * parts):
+    for r in range(units):
         gathered(r)
-        if r + 1 < 2 * parts:
+        if r + 1 < units:
             second(r + 1)
         send_all(r)
-        if r < parts:
-            step_copy(r)
-
-    for r in range(2 * parts):
-        @pl.loop(1, peers)
+        if parts <= r + 2 < units:
+            swap(r + 2).wait_recv()
+            first(r + 2)
+
+    for r in range(units):
+        @pl.loop(1, fan(n_tile, r // parts))
         def _(k):
-            source = holder(me, k, n_tile, r >= parts)
-            home = source if r < parts else copy_of(source)
+            source = feeder(me, k, n_tile, r // parts)
+            home = held_by(source, r // parts)
             pltpu.make_async_remote_copy(
                 src_ref=outgoing[r].at[k], dst_ref=home_rows(home, r),
                 send_sem=t_send.at[r, k], recv_sem=t_recv.at[r, k],
@@ -196,26 +233,27 @@
         near(r, aux, 0, per, 1, down).wait_send()
         near(r, down, 0, half, 2, up).wait_send()
         near(r, up, half, half, 3, down).wait_send()
-        if r < parts:
+        if r >= parts:
             swap(r).wait_send()
 
 
 def fetch_density(density, cols, n_tile, n_aux):
-    units = 2 * len(ROWS)
+    parts = len(ROWS)
+    units = KINDS * parts
     return pl.pallas_call(
         functools.partial(density_kernel, n_tile, n_aux),
         out_shape=jax.ShapeDtypeStruct((n_tile, CAP, TILE, TILE), jnp.float32),
         in_specs=[pl.BlockSpec(memory_space=pltpu.SMEM), pl.BlockSpec(memory_space=pltpu.VMEM)],
         out_specs=pl.BlockSpec(memory_space=pl.ANY),
-        scratch_shapes=[pltpu.VMEM((n_tile, n, TILE), jnp.float32) for n in ROWS * 2]
-        + [pltpu.VMEM((n_tile // 2, CAP, n, TILE), jnp.float32) for n in ROWS * 2]
+        scratch_shapes=[pltpu.VMEM((n_tile, n, TILE), jnp.float32) for n in ROWS * KINDS]
+        + [pltpu.VMEM((fan(n_tile, u // parts), CAP, ROWS[u % parts], TILE), jnp.float32) for u in range(units)]
         + [
             pltpu.SemaphoreType.DMA((units, 4)),
             pltpu.SemaphoreType.DMA((units, 4)),
-            pltpu.SemaphoreType.DMA((len(ROWS),)),
-            pltpu.SemaphoreType.DMA((len(ROWS),)),
-            pltpu.SemaphoreType.DMA((units, n_tile // 2)),
-            pltpu.SemaphoreType.DMA((units, n_tile // 2)),
+            pltpu.SemaphoreType.DMA((units,)),
+            pltpu.SemaphoreType.DMA((units,)),
+            pltpu.SemaphoreType.DMA((units, fan(n_tile, 1))),
+            pltpu.SemaphoreType.DMA((units, fan(n_tile, 1))),
             pltpu.SemaphoreType.DMA((units,)),
         ],
         compiler_params=pltpu.CompilerParams(collective_id=0, has_side_effects=True, vmem_limit_bytes=VMEM_BYTES),
@@ -591,7 +629,7 @@
     sources = packed // n_tile ** 3
     own_source = lax.dynamic_index_in_dim(sources, me, 0, False)
     own_target = lax.dynamic_index_in_dim(targets, me, 0, False)
-    send_cols = jnp.concatenate([slot_columns(sources, columns, me), slot_columns(sources, columns, copy_of(me))])
+    send_cols = jnp.concatenate([slot_columns(sources, columns, held_by(me, kind)) for kind in range(KINDS)])
     places = jnp.arange(n_tile, dtype=jnp.int32)
 
     def order_for(row, copy):

time: 381 us -> 404 us (1.060)
  Pallas kernels: 367 us -> 390 us
    pallas_call x1, Pallas kernels: 141 us -> 161 us  [fetch_density(): pl.pallas_call(functools.partial(density_kernel, n_tile, n_aux), out_shap...]
where the time goes in v8:
time: 404 us; the launch traced here: 399 us
  Pallas kernels  390 us (97%)
  other arithmetic  6.24 us (2%)
    pallas_call x1, Pallas kernels, return_partials(): pl.pallas_call(functools.partial(return_kernel, n_tile, n_aux), out_shape...  191 us
    pallas_call x1, Pallas kernels, fetch_density(): pl.pallas_call(functools.partial(density_kernel, n_tile, n_aux), out_shap...  161 us
    pallas_call x1, Pallas kernels, run_tasks(): pl.pallas_call(functools.partial(task_kernel, aux_funcs // 2), out_shape=...  32.1 us

profile of v8, /device:TPU:22, one launch (start us, length us, event | category | flops | bytes accessed | tf_op | source)
XLA Modules:
  0.0 398.5 jit_solution(4041957788158719764)
XLA Ops:
  0.0 0.6 pad_add_fusion.1.place
  0.7 0.8 slice_bitcast_fusion.1
  1.4 0.1 iota_compare_fusion.7
  1.5 0.1 iota_compare_fusion.9
  1.6 0.9 add_reduce_fusion
  2.5 0.1 reshape.370
  2.7 0.3 and_select_fusion.1
  2.9 0.1 copy.41
  3.0 0.2 and_select_fusion
  3.2 0.1 copy.47
  3.2 0.1 fusion.5
  3.3 0.1 broadcast_compare_fusion.1
  3.4 0.2 convert_reduce_fusion.7
  3.6 0.2 convert_reduce_fusion.6
  3.8 0.6 pad_add_fusion.table
  4.4 0.1 copy.46
  4.5 0.1 copy.40
  4.5 0.4 convert_reduce_fusion
  4.9 0.1 copy.48
  5.0 0.2 select_reduce_fusion.5
  5.2 0.1 add_add_fusion
  5.3 0.1 copy.42
  5.4 0.2 select_reduce_fusion.9
  5.6 0.1 select_reduce_fusion.7
  5.8 0.1 select_reduce_fusion.11
  5.9 0.1 copy.44
  6.0 0.1 sub.148
  6.1 0.1 copy.45
  6.2 0.1 sub.155
  6.3 0.2 fusion.14
  6.5 0.2 convert_reduce_fusion.2
  6.7 0.1 fusion.13
  6.8 0.1 select_reduce_fusion.6
  6.9 0.2 fusion.12
  7.1 0.2 convert_reduce_fusion.4
  7.3 0.1 fusion.11
  7.4 0.1 select_reduce_fusion.10
  7.6 0.6 concatenate.14.order_ref
  8.2 0.1 copy.50
  8.3 0.7 broadcast_maximum_fusion.cols_ref
  9.0 160.6 %fetch_density.1 = f32[64,2,128,128]{3,2,1,0:T(8,128)} custom-call(s32[192,2]{1,0:T(8,128)} %broadcast_maximum_fusion.cols_ref, f32[128,2048]{1,0:T(8,128)} %dens_ref.1), custom_call_target="tpu_custom_call" | custom-call | tf_op jit(solution)/shard_map/fetch_density/pallas_call | solution.py:243
  169.6 32.1 %run_tasks.1 = f32[128,128,128]{2,1,0:T(8,128)} custom-call(s32[4,32]{1,0:T(4,128)} %pad_add_fusion.table, f32[128,128,128]{2,1,0:T(8,128)} %bitcast.59, f32[6,2048,128]{2,1,0:T(8,128)} %bitcast.60), custom_call_target="tpu_custom_call" | custom-call | tf_op jit(solution)/shard_map/run_tasks/pallas_call | solution.py:300
  201.8 191.0 %return_partials.1 = (f32[16,128,128]{2,1,0:T(8,128)}, f32[16,128,128]{2,1,0:T(8,128)}) custom-call(s32[8,64]{1,0:T(8,128)} %concatenate.14.order_ref, f32[64,2,128,128]{3,2,1,0:T(8,128)} %bitcast.58), custom_call_target="tpu_custom_call" | custom-call | tf_op jit(solution)/shard_map/return_partials/pallas_call | solution.py:537
  392.7 5.8 %finish.1 = f32[128,2048]{1,0:T(8,128)} custom-call(s32[2]{0:T(128)} %pad_add_fusion.1.place, f32[16,128,128]{2,1,0:T(8,128)} %get-tuple-element.7.own_ref, f32[16,128,128]{2,1,0:T(8,128)} %get-tuple-element.8.mirror_ref, f32[8192,128]{1,0:T(8,128)} %right_ref.1, f32[8192,128]{1,0:T(8,128)} %right_ref.1), custom_call_target="tpu_custom_call" | custom-call | tf_op jit(solution)/shard_map/finish/pallas_call | solution.py:586
  (30 shorter events, 0.2 us)

commit v9 on v7

--- a/solution.py
+++ b/solution.py
@@ -16,7 +16,7 @@
 ROWS = (32, 48, 48)
 SPANS = [(sum(ROWS[:r]), n) for r, n in enumerate(ROWS)]
 BACK = (48, 40, 24, 16)
-AHEAD = 2
+AHEAD = 3
 BACK_SPANS = [(sum(BACK[:r]), n) for r, n in enumerate(BACK)]
 
 
@@ -379,8 +379,6 @@
                 device_id={"tile": served(me, k, n_tile, u % 2 == 0), "aux": aux}, device_id_type=MESH).wait_recv()
 
         own(u).wait()
-        if u + AHEAD < units:
-            begin(u + AHEAD)
 
         def add(i, carry):
             for v in range(4):
@@ -457,6 +455,8 @@
         if u > 0:
             conclude(u - 1)
         pass_on(u)
+        if u + AHEAD < units:
+            begin(u + AHEAD)
     conclude(units - 1)
 
     for u in range(units):

time: 381 us -> 383 us (level)
  no operation moved by 1% of the time
where the time goes in v9:
time: 383 us; the launch traced here: 375 us
  Pallas kernels  366 us (96%)
  other arithmetic  6.15 us (2%)
    pallas_call x1, Pallas kernels, return_partials(): pl.pallas_call(functools.partial(return_kernel, n_tile, n_aux), out_shape...  188 us
    pallas_call x1, Pallas kernels, fetch_density(): pl.pallas_call(functools.partial(density_kernel, n_tile, n_aux), out_shap...  141 us
    pallas_call x1, Pallas kernels, run_tasks(): pl.pallas_call(functools.partial(task_kernel, aux_funcs // 2), out_shape=...  32.1 us

profile of v9, /device:TPU:22, one launch (start us, length us, event | category | flops | bytes accessed | tf_op | source)
XLA Modules:
  0.0 375.1 jit_solution(8232366902318379323)
XLA Ops:
  0.0 0.6 pad_add_fusion.1.place
  0.7 0.8 slice_bitcast_fusion.1
  1.4 0.1 iota_compare_fusion.7
  1.5 0.1 iota_compare_fusion.9
  1.6 0.9 add_reduce_fusion
  2.5 0.1 reshape.352
  2.7 0.3 and_select_fusion.1
  2.9 0.1 copy.37
  3.0 0.2 and_select_fusion
  3.2 0.1 copy.43
  3.2 0.1 fusion.5
  3.3 0.1 broadcast_compare_fusion.2
  3.4 0.2 convert_reduce_fusion.7
  3.6 0.2 convert_reduce_fusion.6
  3.8 0.6 pad_add_fusion.table
  4.4 0.1 copy.42
  4.4 0.1 copy.36
  4.5 0.4 convert_reduce_fusion
  4.9 0.1 copy.44
  5.0 0.2 select_reduce_fusion.3
  5.2 0.1 add_add_fusion.2
  5.2 0.1 copy.38
  5.3 0.2 select_reduce_fusion.7
  5.5 0.1 select_reduce_fusion.5
  5.7 0.1 select_reduce_fusion.9
  5.8 0.1 copy.40
  5.9 0.1 sub.132
  6.0 0.1 copy.41
  6.1 0.1 sub.139
  6.2 0.2 fusion.14
  6.4 0.2 convert_reduce_fusion.2
  6.6 0.1 fusion.13
  6.7 0.1 select_reduce_fusion.4
  6.9 0.2 fusion.12
  7.1 0.2 convert_reduce_fusion.4
  7.3 0.1 fusion.11
  7.4 0.1 select_reduce_fusion.8
  7.5 0.6 concatenate.14.order_ref
  8.1 0.1 copy.46
  8.2 0.6 broadcast_maximum_fusion.cols_ref
  8.9 140.8 %fetch_density.1 = f32[64,2,128,128]{3,2,1,0:T(8,128)} custom-call(s32[128,2]{1,0:T(8,128)} %broadcast_maximum_fusion.cols_ref, f32[128,2048]{1,0:T(8,128)} %dens_ref.1), custom_call_target="tpu_custom_call" | custom-call | tf_op jit(solution)/shard_map/fetch_density/pallas_call | solution.py:205
  149.6 32.1 %run_tasks.1 = f32[128,128,128]{2,1,0:T(8,128)} custom-call(s32[4,32]{1,0:T(4,128)} %pad_add_fusion.table, f32[128,128,128]{2,1,0:T(8,128)} %bitcast.55, f32[6,2048,128]{2,1,0:T(8,128)} %bitcast.56), custom_call_target="tpu_custom_call" | custom-call | tf_op jit(solution)/shard_map/run_tasks/pallas_call | solution.py:262
  181.8 187.5 %return_partials.1 = (f32[16,128,128]{2,1,0:T(8,128)}, f32[16,128,128]{2,1,0:T(8,128)}) custom-call(s32[8,64]{1,0:T(8,128)} %concatenate.14.order_ref, f32[64,2,128,128]{3,2,1,0:T(8,128)} %bitcast.54), custom_call_target="tpu_custom_call" | custom-call | tf_op jit(solution)/shard_map/return_partials/pallas_call | solution.py:499
  369.3 5.8 %finish.1 = f32[128,2048]{1,0:T(8,128)} custom-call(s32[2]{0:T(128)} %pad_add_fusion.1.place, f32[16,128,128]{2,1,0:T(8,128)} %get-tuple-element.7.own_ref, f32[16,128,128]{2,1,0:T(8,128)} %get-tuple-element.8.mirror_ref, f32[8192,128]{1,0:T(8,128)} %right_ref.1, f32[8192,128]{1,0:T(8,128)} %right_ref.1), custom_call_target="tpu_custom_call" | custom-call | tf_op jit(solution)/shard_map/finish/pallas_call | solution.py:548
  (28 shorter events, 0.2 us)

commit v10 on v7

--- a/solution.py
+++ b/solution.py
@@ -13,7 +13,7 @@
 RING = 8
 CORES = 2
 ORDER = 13
-ROWS = (32, 48, 48)
+ROWS = (48, 80)
 SPANS = [(sum(ROWS[:r]), n) for r, n in enumerate(ROWS)]
 BACK = (48, 40, 24, 16)
 AHEAD = 2
@@ -542,7 +542,7 @@
 
 def finish(place, own, mirror, orthogonalizers):
     per = own.shape[0]
-    group = 4
+    group = 8
     steps = per // group
     tile = pl.BlockSpec((group, TILE, TILE), lambda j, t: (j, 0, 0))
     return pl.pallas_call(

time: 381 us -> 380 us (level)
  no operation moved by 1% of the time
where the time goes in v10:
time: 380 us; the launch traced here: 375 us
  Pallas kernels  367 us (97%)
  other arithmetic  6.15 us (2%)
    pallas_call x1, Pallas kernels, return_partials(): pl.pallas_call(functools.partial(return_kernel, n_tile, n_aux), out_shape...  190 us
    pallas_call x1, Pallas kernels, fetch_density(): pl.pallas_call(functools.partial(density_kernel, n_tile, n_aux), out_shap...  140 us
    pallas_call x1, Pallas kernels, run_tasks(): pl.pallas_call(functools.partial(task_kernel, aux_funcs // 2), out_shape=...  32.1 us

profile of v10, /device:TPU:22, one launch (start us, length us, event | category | flops | bytes accessed | tf_op | source)
XLA Modules:
  0.0 375.5 jit_solution(17176499271946911543)
XLA Ops:
  0.0 0.6 pad_add_fusion.1.place
  0.7 0.8 slice_bitcast_fusion.1
  1.4 0.1 iota_compare_fusion.7
  1.5 0.1 iota_compare_fusion.9
  1.6 0.9 add_reduce_fusion
  2.5 0.1 reshape.352
  2.7 0.3 and_select_fusion.1
  2.9 0.1 copy.37
  3.0 0.2 and_select_fusion
  3.2 0.1 copy.43
  3.2 0.1 fusion.5
  3.3 0.1 broadcast_compare_fusion.2
  3.4 0.2 convert_reduce_fusion.7
  3.6 0.2 convert_reduce_fusion.6
  3.8 0.6 pad_add_fusion.table
  4.4 0.1 copy.42
  4.4 0.1 copy.36
  4.5 0.4 convert_reduce_fusion
  4.9 0.1 copy.44
  5.0 0.2 select_reduce_fusion.3
  5.2 0.1 add_add_fusion.2
  5.2 0.1 copy.38
  5.3 0.2 select_reduce_fusion.7
  5.5 0.1 select_reduce_fusion.5
  5.7 0.1 select_reduce_fusion.9
  5.8 0.1 copy.40
  5.9 0.1 sub.132
  6.0 0.1 copy.41
  6.1 0.1 sub.139
  6.2 0.2 fusion.14
  6.4 0.2 convert_reduce_fusion.2
  6.6 0.1 fusion.13
  6.7 0.1 select_reduce_fusion.4
  6.9 0.2 fusion.12
  7.1 0.2 convert_reduce_fusion.4
  7.3 0.1 fusion.11
  7.4 0.1 select_reduce_fusion.8
  7.5 0.6 concatenate.14.order_ref
  8.1 0.1 copy.46
  8.2 0.6 broadcast_maximum_fusion.cols_ref
  8.9 139.9 %fetch_density.1 = f32[64,2,128,128]{3,2,1,0:T(8,128)} custom-call(s32[128,2]{1,0:T(8,128)} %broadcast_maximum_fusion.cols_ref, f32[128,2048]{1,0:T(8,128)} %dens_ref.1), custom_call_target="tpu_custom_call" | custom-call | tf_op jit(solution)/shard_map/fetch_density/pallas_call | solution.py:205
  148.8 32.1 %run_tasks.1 = f32[128,128,128]{2,1,0:T(8,128)} custom-call(s32[4,32]{1,0:T(4,128)} %pad_add_fusion.table, f32[128,128,128]{2,1,0:T(8,128)} %bitcast.55, f32[6,2048,128]{2,1,0:T(8,128)} %bitcast.56), custom_call_target="tpu_custom_call" | custom-call | tf_op jit(solution)/shard_map/run_tasks/pallas_call | solution.py:262
  180.9 189.7 %return_partials.1 = (f32[16,128,128]{2,1,0:T(8,128)}, f32[16,128,128]{2,1,0:T(8,128)}) custom-call(s32[8,64]{1,0:T(8,128)} %concatenate.14.order_ref, f32[64,2,128,128]{3,2,1,0:T(8,128)} %bitcast.54), custom_call_target="tpu_custom_call" | custom-call | tf_op jit(solution)/shard_map/return_partials/pallas_call | solution.py:499
  370.6 4.8 %finish.1 = f32[128,2048]{1,0:T(8,128)} custom-call(s32[2]{0:T(128)} %pad_add_fusion.1.place, f32[16,128,128]{2,1,0:T(8,128)} %get-tuple-element.7.own_ref, f32[16,128,128]{2,1,0:T(8,128)} %get-tuple-element.8.mirror_ref, f32[8192,128]{1,0:T(8,128)} %right_ref.1, f32[8192,128]{1,0:T(8,128)} %right_ref.1), custom_call_target="tpu_custom_call" | custom-call | tf_op jit(solution)/shard_map/finish/pallas_call | solution.py:548
  (28 shorter events, 0.2 us)
